TPU v7x, 512 devices: a whole 4x4x16 slice. The times are simulated.
512 devices in a mesh: gx: 64 (over z, x_hi, core), gy: 8 (over y, x_lo).
Axes of the slice: x: 4 (x_hi: 2, x_lo: 2; x = x_hi * 2 + x_lo), y: 4, z: 16, core: 2. Of those that a mesh axis runs over, the one named last changes fastest.
Arguments:
- iterate: float32 [32, 1536, 1024], P(None, 'gx', 'gy'), may hold values from -6 to 6
- source: float32 [32, 1536, 1024], P(None, 'gx', 'gy'), may hold values from -8 to 8
- conduct: float32 [32, 1536, 1024], P(None, 'gx', 'gy'), may hold values from 0.2 to 5
Outputs:
- updated: float32 [32, 1536, 1024], P(None, 'gx', 'gy')
All inputs are finite; a program needn't handle non-finite values.
Results may differ from a plain program's by a relative error of at most 0.000041.
Values sent between devices are 32-bit elements; how exact they have to be, the bound alone decides.
A program may use at most 64 MiB of HBM per device.

v0:
```python
import jax
import jax.numpy as jnp
from jax import lax
from jax.sharding import PartitionSpec as P

SWEEPS = 3
COARSE_SWEEPS = 4
COARSEN = 8


SHIFT = 0.1
LMIN = 0.3
LMAX = 2.0
OMEGA = 0.8


def extended(x, sides, width):
    for axis, dim in sides:
        size, length = (lax.axis_size(axis), x.shape[dim])
        up = [(i, (i + 1) % size) for i in range(size)]
        down = [(j, i) for i, j in up]
        last = lax.slice_in_dim(x, length - width, length, axis=dim)
        first = lax.slice_in_dim(x, 0, width, axis=dim)
        before = lax.ppermute(last, axis, up)
        after = lax.ppermute(first, axis, down)
        x = jnp.concatenate([before, x, after], axis=dim)
    return x


def pairs_of(field, cond):
    centre = field[:, 1:-1, 1:-1]
    middle = cond[:, 1:-1, 1:-1]
    listed = [
        (jnp.roll(centre, 1, 0), jnp.roll(middle, 1, 0)),
        (jnp.roll(centre, -1, 0), jnp.roll(middle, -1, 0)),
        (field[:, 2:, 1:-1], cond[:, 2:, 1:-1]),
        (field[:, :-2, 1:-1], cond[:, :-2, 1:-1]),
        (field[:, 1:-1, 2:], cond[:, 1:-1, 2:]),
        (field[:, 1:-1, :-2], cond[:, 1:-1, :-2]),
    ]
    return (centre, middle, listed)


def operate_pad(field, cond, factor):
    centre, middle, listed = pairs_of(field, cond)
    summed = jnp.zeros_like(centre)
    for near_v, near_c in listed:
        summed = summed + 0.5 * (middle + near_c) * (centre - near_v)
    return SHIFT * centre + factor * summed


def diagonal_pad(cond, factor):
    centre, middle, listed = pairs_of(cond, cond)
    summed = jnp.zeros_like(middle)
    for near_v, near_c in listed:
        summed = summed + 0.5 * (middle + near_c)
    return SHIFT + factor * summed


def restrict(values):
    depth, width_x, width_y = values.shape
    blocks = values.reshape(
        depth // COARSEN, COARSEN, width_x // COARSEN, COARSEN, width_y // COARSEN, COARSEN
    )
    return jnp.mean(blocks, axis=(1, 3, 5))


def prolong(values):
    depth, width_x, width_y = values.shape
    spread = jnp.broadcast_to(
        values[:, None, :, None, :, None], (depth, COARSEN, width_x, COARSEN, width_y, COARSEN)
    )
    return spread.reshape(depth * COARSEN, width_x * COARSEN, width_y * COARSEN)


def body(iterate, source, conduct):
    theta = (LMAX + LMIN) / 2.0
    delta = (LMAX - LMIN) / 2.0
    sigma = theta / delta
    rho_now = 1.0 / sigma
    stacked = jnp.stack([iterate, conduct])
    padded = extended(stacked, (("gx", 2), ("gy", 3)), 1)
    cond_pad = padded[1]
    residual = source - operate_pad(padded[0], cond_pad, 1.0)
    diag_fine = diagonal_pad(cond_pad, 1.0)
    correction = jnp.zeros_like(residual)
    remainder = residual
    direction = residual / (theta * diag_fine)
    for sweep_index in range(SWEEPS):
        dir_pad = extended(direction, (("gx", 1), ("gy", 2)), 1)
        image = operate_pad(dir_pad, cond_pad, 1.0)
        correction = correction + direction
        remainder = remainder - image
        rho_next = 1.0 / (2.0 * sigma - rho_now)
        direction = rho_next * rho_now * direction + 2.0 * rho_next / delta * remainder / diag_fine
        rho_now = rho_next
    correction = correction + direction
    coarse_rhs = restrict(residual)
    coarse_cond = restrict(conduct)
    cond_wide = extended(coarse_cond, (("gx", 1), ("gy", 2)), 1)
    diag_coarse = diagonal_pad(cond_wide, 1.0 / 64.0)
    coarse = OMEGA * coarse_rhs / diag_coarse
    for sweep_index in range(COARSE_SWEEPS - 1):
        coarse_wide = extended(coarse, (("gx", 1), ("gy", 2)), 1)
        coarse = (
            coarse
            + OMEGA * (coarse_rhs - operate_pad(coarse_wide, cond_wide, 1.0 / 64.0)) / diag_coarse
        )
    return iterate + correction + prolong(coarse)


def solution(mesh):
    return jax.shard_map(
        body,
        mesh=mesh,
        in_specs=(P(None, "gx", "gy"), P(None, "gx", "gy"), P(None, "gx", "gy")),
        out_specs=P(None, "gx", "gy"),
        check_vma=False,
    )
```

profile of v0, /device:TPU:8, one launch (start us, length us, event | category | flops | bytes accessed | tf_op | source)
XLA Modules:
  0.0 238.7 jit_solution(15325518953496496094)
XLA Ops:
  1.1 13.3 %collective-permute-start.1 = (f32[2,32,1,128]{3,2,1,0:T(1,128)S(1)}, f32[2,32,1,128]{3,2,1,0:T(1,128)S(1)}, u32[]{:S(2)}, u32[]{:S(2)}) collective-permute-start(f32[2,32,1,128]{3,2,1,0:T(1,128)S(1)} %get-tuple-element.36), channel_id=1, source_target_pairs={{8,0},{16,8},{24,16},{32,24},{40,32},{48,40},{56,48},{64,56},{72,6... | collective-permute-start | bytes 98312 | tf_op jit(solution)/shard_map/ppermute | solution.py:25
  16.4 5.8 %reshape.11 = f32[4,8,3,8,16,8]{5,4,3,2,1,0:T(8,128)} reshape(f32[32,24,128]{2,1,0:T(8,128)} %param.5) | data formatting | bytes 786432 | tf_op jit(solution)/shard_map/reshape | solution.py:62
  22.2 3.4 %reduce_sum.19 = f32[4,3,16]{2,1,0:T(4,128)S(1)} reduce(f32[4,8,3,8,16,8]{5,4,3,2,1,0:T(8,128)} %reshape.11, f32[]{:T(128)} %constant.11.clone.1), dimensions={1,3,5}, to_apply=%region_1.2 | reduce | flops 98112 | bytes 393988 | tf_op jit(solution)/shard_map/reduce_sum | solution.py:65
  25.6 7.3 %collective-permute-start.16 = (f32[4,1,16]{2,1,0:T(1,128)S(1)}, f32[4,1,16]{2,1,0:T(1,128)S(1)}, u32[]{:S(2)}, u32[]{:S(2)}) collective-permute-start(f32[4,1,16]{2,1,0:T(1,128)S(1)} %get-tuple-element.92), channel_id=1, source_target_pairs={{8,0},{16,8},{24,16},{32,24},{40,32},{48,40},{56,48},{64,56},{72,6... | collective-permute-start | bytes 776 | tf_op jit(solution)/shard_map/ppermute | solution.py:25
  36.0 5.4 %collective-permute-done.17 = f32[4,1,16]{2,1,0:T(1,128)S(1)} collective-permute-done((f32[4,1,16]{2,1,0:T(1,128)S(1)}, f32[4,1,16]{2,1,0:T(1,128)S(1)}, u32[]{:S(2)}, u32[]{:S(2)}) %collective-permute-start.17) | collective-permute-done | bytes 288 | tf_op jit(solution)/shard_map/ppermute | solution.py:24
  45.7 3.4 %collective-permute-start.2 = (f32[2,32,26,1]{1,0,3,2:T(2,128)S(1)}, f32[2,32,26,1]{1,0,3,2:T(2,128)S(1)}, u32[]{:S(2)}, u32[]{:S(2)}) collective-permute-start(f32[2,32,26,1]{1,0,3,2:T(2,128)S(1)} %copy.4), channel_id=1, source_target_pairs={{0,1},{1,2},{2,3},{3,4},{4,5},{5,6},{6,7},{7,0},{8,9},{9,10},{10,1... | collective-permute-start | bytes 19976 | tf_op jit(solution)/shard_map/ppermute | solution.py:24
  49.8 3.3 %collective-permute-start.18 = (f32[4,5,1]{2,1,0:T(8,128)}, f32[4,5,1]{2,1,0:T(8,128)}, u32[]{:S(2)}, u32[]{:S(2)}) collective-permute-start(f32[4,5,1]{2,1,0:T(8,128)} %get-tuple-element.68), channel_id=1, source_target_pairs={{1,0},{2,1},{3,2},{4,3},{5,4},{6,5},{7,6},{0,7},{9,8},{10,9},{11,1... | collective-permute-start | bytes 248 | tf_op jit(solution)/shard_map/ppermute | solution.py:25
  60.9 5.0 %reshape.10 = f32[4,8,3,8,16,8]{5,4,3,2,1,0:T(8,128)} reshape(f32[32,24,128]{2,1,0:T(8,128)S(1)} %get-tuple-element.11) | data formatting | bytes 786432 | tf_op jit(solution)/shard_map/reshape | solution.py:62
  65.9 3.3 %reduce_sum.18 = f32[4,3,16]{2,1,0:T(4,128)S(1)} reduce(f32[4,8,3,8,16,8]{5,4,3,2,1,0:T(8,128)} %reshape.10, f32[]{:T(128)} %constant.11.clone.1), dimensions={1,3,5}, to_apply=%region_0.1 | reduce | flops 98112 | bytes 393988 | tf_op jit(solution)/shard_map/reduce_sum | solution.py:65
  76.1 6.8 %collective-permute-start.4 = (f32[32,1,128]{2,1,0:T(1,128)S(1)}, f32[32,1,128]{2,1,0:T(1,128)S(1)}, u32[]{:S(2)}, u32[]{:S(2)}) collective-permute-start(f32[32,1,128]{2,1,0:T(1,128)S(1)} %get-tuple-element.60), channel_id=1, source_target_pairs={{8,0},{16,8},{24,16},{32,24},{40,32},{48,40},{56,48},{64,56},{72,6... | collective-permute-start | bytes 49160 | tf_op jit(solution)/shard_map/ppermute | solution.py:25
  84.9 4.3 %collective-permute-start.23 = (f32[4,5,1]{2,1,0:T(8,128)S(1)}, f32[4,5,1]{2,1,0:T(8,128)S(1)}, u32[]{:S(2)}, u32[]{:S(2)}) collective-permute-start(f32[4,5,1]{2,1,0:T(8,128)S(1)} %get-tuple-element.66), channel_id=1, source_target_pairs={{0,1},{1,2},{2,3},{3,4},{4,5},{5,6},{6,7},{7,0},{8,9},{9,10},{10,1... | collective-permute-start | bytes 248 | tf_op jit(solution)/shard_map/ppermute | solution.py:24
  91.6 3.2 %collective-permute-done.22 = f32[4,5,1]{2,1,0:T(8,128)S(1)} collective-permute-done((f32[4,5,1]{2,1,0:T(8,128)S(1)}, f32[4,5,1]{2,1,0:T(8,128)S(1)}, u32[]{:S(2)}, u32[]{:S(2)}) %collective-permute-start.22) | collective-permute-done | bytes 112 | tf_op jit(solution)/shard_map/ppermute | solution.py:25
  95.6 6.4 %collective-permute-start.24 = (f32[4,1,16]{2,1,0:T(1,128)S(1)}, f32[4,1,16]{2,1,0:T(1,128)S(1)}, u32[]{:S(2)}, u32[]{:S(2)}) collective-permute-start(f32[4,1,16]{2,1,0:T(1,128)S(1)} %get-tuple-element.80), channel_id=1, source_target_pairs={{8,0},{16,8},{24,16},{32,24},{40,32},{48,40},{56,48},{64,56},{72,6... | collective-permute-start | bytes 776 | tf_op jit(solution)/shard_map/ppermute | solution.py:25
  104.0 6.6 %collective-permute-done.25 = f32[4,1,16]{2,1,0:T(1,128)S(1)} collective-permute-done((f32[4,1,16]{2,1,0:T(1,128)S(1)}, f32[4,1,16]{2,1,0:T(1,128)S(1)}, u32[]{:S(2)}, u32[]{:S(2)}) %collective-permute-start.25) | collective-permute-done | bytes 288 | tf_op jit(solution)/shard_map/ppermute | solution.py:24
  113.3 4.1 %collective-permute-start.26 = (f32[4,5,1]{2,1,0:T(8,128)S(1)}, f32[4,5,1]{2,1,0:T(8,128)S(1)}, u32[]{:S(2)}, u32[]{:S(2)}) collective-permute-start(f32[4,5,1]{2,1,0:T(8,128)S(1)} %get-tuple-element.63), channel_id=1, source_target_pairs={{1,0},{2,1},{3,2},{4,3},{5,4},{6,5},{7,6},{0,7},{9,8},{10,9},{11,1... | collective-permute-start | bytes 248 | tf_op jit(solution)/shard_map/ppermute | solution.py:25
  123.8 6.1 %collective-permute-done.29 = f32[4,1,16]{2,1,0:T(1,128)S(1)} collective-permute-done((f32[4,1,16]{2,1,0:T(1,128)S(1)}, f32[4,1,16]{2,1,0:T(1,128)S(1)}, u32[]{:S(2)}, u32[]{:S(2)}) %collective-permute-start.29) | collective-permute-done | bytes 288 | tf_op jit(solution)/shard_map/ppermute | solution.py:24
  129.9 4.8 %collective-permute-start.31 = (f32[4,5,1]{2,1,0:T(8,128)S(1)}, f32[4,5,1]{2,1,0:T(8,128)S(1)}, u32[]{:S(2)}, u32[]{:S(2)}) collective-permute-start(f32[4,5,1]{2,1,0:T(8,128)S(1)} %get-tuple-element.62), channel_id=1, source_target_pairs={{0,1},{1,2},{2,3},{3,4},{4,5},{5,6},{6,7},{7,0},{8,9},{9,10},{10,1... | collective-permute-start | bytes 248 | tf_op jit(solution)/shard_map/ppermute | solution.py:24
  139.2 4.2 %collective-permute-start.7 = (f32[32,26,1]{2,1,0:T(8,128)}, f32[32,26,1]{2,1,0:T(8,128)}, u32[]{:S(2)}, u32[]{:S(2)}) collective-permute-start(f32[32,26,1]{2,1,0:T(8,128)} %get-tuple-element.42), channel_id=1, source_target_pairs={{0,1},{1,2},{2,3},{3,4},{4,5},{5,6},{6,7},{7,0},{8,9},{9,10},{10,1... | collective-permute-start | bytes 9992 | tf_op jit(solution)/shard_map/ppermute | solution.py:24
  143.3 2.8 %collective-permute-start.6 = (f32[32,26,1]{2,1,0:T(8,128)}, f32[32,26,1]{2,1,0:T(8,128)}, u32[]{:S(2)}, u32[]{:S(2)}) collective-permute-start(f32[32,26,1]{2,1,0:T(8,128)} %get-tuple-element.41), channel_id=1, source_target_pairs={{1,0},{2,1},{3,2},{4,3},{5,4},{6,5},{7,6},{0,7},{9,8},{10,9},{11,1... | collective-permute-start | bytes 9992 | tf_op jit(solution)/shard_map/ppermute | solution.py:25
  146.3 3.2 %broadcast_in_dim.2 = f32[4,8,3,8,16,8]{5,4,3,2,1,0:T(8,128)} broadcast(f32[4,3,16]{2,1,0:T(4,128)S(1)} %fusion.84), dimensions={0,2,4} | broadcast | bytes 393984 | tf_op jit(solution)/shard_map/broadcast_in_dim | solution.py:70
  149.6 5.9 %reshape.12 = f32[32,24,128]{2,1,0:T(8,128)} reshape(f32[4,8,3,8,16,8]{5,4,3,2,1,0:T(8,128)} %broadcast_in_dim.2) | data formatting | bytes 786432 | tf_op jit(solution)/shard_map/reshape | solution.py:73
  157.0 7.5 %collective-permute-done.6 = f32[32,26,1]{2,1,0:T(8,128)} collective-permute-done((f32[32,26,1]{2,1,0:T(8,128)}, f32[32,26,1]{2,1,0:T(8,128)}, u32[]{:S(2)}, u32[]{:S(2)}) %collective-permute-start.6) | collective-permute-done | bytes 3360 | tf_op jit(solution)/shard_map/ppermute | solution.py:25
  171.1 6.3 %collective-permute-done.9 = f32[32,1,128]{2,1,0:T(1,128)S(1)} collective-permute-done((f32[32,1,128]{2,1,0:T(1,128)S(1)}, f32[32,1,128]{2,1,0:T(1,128)S(1)}, u32[]{:S(2)}, u32[]{:S(2)}) %collective-permute-start.9) | collective-permute-done | bytes 16416 | tf_op jit(solution)/shard_map/ppermute | solution.py:24
  177.7 3.7 %collective-permute-start.11 = (f32[32,26,1]{2,1,0:T(8,128)S(1)}, f32[32,26,1]{2,1,0:T(8,128)S(1)}, u32[]{:S(2)}, u32[]{:S(2)}) collective-permute-start(f32[32,26,1]{2,1,0:T(8,128)S(1)} %get-tuple-element.40), channel_id=1, source_target_pairs={{0,1},{1,2},{2,3},{3,4},{4,5},{5,6},{6,7},{7,0},{8,9},{9,10},{10,1... | collective-permute-start | bytes 9992 | tf_op jit(solution)/shard_map/ppermute | solution.py:24
  181.4 3.1 %collective-permute-start.10 = (f32[32,26,1]{2,1,0:T(8,128)S(1)}, f32[32,26,1]{2,1,0:T(8,128)S(1)}, u32[]{:S(2)}, u32[]{:S(2)}) collective-permute-start(f32[32,26,1]{2,1,0:T(8,128)S(1)} %get-tuple-element.39), channel_id=1, source_target_pairs={{1,0},{2,1},{3,2},{4,3},{5,4},{6,5},{7,6},{0,7},{9,8},{10,9},{11,1... | collective-permute-start | bytes 9992 | tf_op jit(solution)/shard_map/ppermute | solution.py:25
  184.5 10.3 %collective-permute-done.11 = f32[32,26,1]{2,1,0:T(8,128)S(1)} collective-permute-done((f32[32,26,1]{2,1,0:T(8,128)S(1)}, f32[32,26,1]{2,1,0:T(8,128)S(1)}, u32[]{:S(2)}, u32[]{:S(2)}) %collective-permute-start.11) | collective-permute-done | bytes 3360 | tf_op jit(solution)/shard_map/ppermute | solution.py:24
  194.8 6.6 %collective-permute-done.10 = f32[32,26,1]{2,1,0:T(8,128)S(1)} collective-permute-done((f32[32,26,1]{2,1,0:T(8,128)S(1)}, f32[32,26,1]{2,1,0:T(8,128)S(1)}, u32[]{:S(2)}, u32[]{:S(2)}) %collective-permute-start.10) | collective-permute-done | bytes 3360 | tf_op jit(solution)/shard_map/ppermute | solution.py:25
  206.8 6.3 %collective-permute-done.13 = f32[32,1,128]{2,1,0:T(1,128)S(1)} collective-permute-done((f32[32,1,128]{2,1,0:T(1,128)S(1)}, f32[32,1,128]{2,1,0:T(1,128)S(1)}, u32[]{:S(2)}, u32[]{:S(2)}) %collective-permute-start.13) | collective-permute-done | bytes 16416 | tf_op jit(solution)/shard_map/ppermute | solution.py:24
  213.3 3.7 %collective-permute-start.15 = (f32[32,26,1]{2,1,0:T(8,128)S(1)}, f32[32,26,1]{2,1,0:T(8,128)S(1)}, u32[]{:S(2)}, u32[]{:S(2)}) collective-permute-start(f32[32,26,1]{2,1,0:T(8,128)S(1)} %get-tuple-element.38), channel_id=1, source_target_pairs={{0,1},{1,2},{2,3},{3,4},{4,5},{5,6},{6,7},{7,0},{8,9},{9,10},{10,1... | collective-permute-start | bytes 9992 | tf_op jit(solution)/shard_map/ppermute | solution.py:24
  217.0 3.1 %collective-permute-start.14 = (f32[32,26,1]{2,1,0:T(8,128)S(1)}, f32[32,26,1]{2,1,0:T(8,128)S(1)}, u32[]{:S(2)}, u32[]{:S(2)}) collective-permute-start(f32[32,26,1]{2,1,0:T(8,128)S(1)} %get-tuple-element.37), channel_id=1, source_target_pairs={{1,0},{2,1},{3,2},{4,3},{5,4},{6,5},{7,6},{0,7},{9,8},{10,9},{11,1... | collective-permute-start | bytes 9992 | tf_op jit(solution)/shard_map/ppermute | solution.py:25
  220.1 10.3 %collective-permute-done.15 = f32[32,26,1]{2,1,0:T(8,128)S(1)} collective-permute-done((f32[32,26,1]{2,1,0:T(8,128)S(1)}, f32[32,26,1]{2,1,0:T(8,128)S(1)}, u32[]{:S(2)}, u32[]{:S(2)}) %collective-permute-start.15) | collective-permute-done | bytes 3360 | tf_op jit(solution)/shard_map/ppermute | solution.py:24
  230.4 6.7 %collective-permute-done.14 = f32[32,26,1]{2,1,0:T(8,128)S(1)} collective-permute-done((f32[32,26,1]{2,1,0:T(8,128)S(1)}, f32[32,26,1]{2,1,0:T(8,128)S(1)}, u32[]{:S(2)}, u32[]{:S(2)}) %collective-permute-start.14) | collective-permute-done | bytes 3360 | tf_op jit(solution)/shard_map/ppermute | solution.py:25
  (119 shorter events, 62.0 us)
Async XLA Ops:
  1.1 40.3 %collective-permute-start.1 = (f32[2,32,1,128]{3,2,1,0:T(1,128)S(1)}, f32[2,32,1,128]{3,2,1,0:T(1,128)S(1)}, u32[]{:S(2)}, u32[]{:S(2)}) collective-permute-start(f32[2,32,1,128]{3,2,1,0:T(1,128)S(1)} %get-tuple-element.36), channel_id=1, source_target_pairs={{8,0},{16,8},{24,16},{32,24},{40,32},{48,40},{56,48},{64,56},{72,6... | collective-permute-start | bytes 98312 | tf_op jit(solution)/shard_map/ppermute | solution.py:25
  14.5 27.0 %collective-permute-start = (f32[2,32,1,128]{3,2,1,0:T(1,128)S(1)}, f32[2,32,1,128]{3,2,1,0:T(1,128)S(1)}, u32[]{:S(2)}, u32[]{:S(2)}) collective-permute-start(f32[2,32,1,128]{3,2,1,0:T(1,128)S(1)} %get-tuple-element.35), channel_id=1, source_target_pairs={{0,8},{8,16},{16,24},{24,32},{32,40},{40,48},{48,56},{56,64},{64,7... | collective-permute-start | bytes 98312 | tf_op jit(solution)/shard_map/ppermute | solution.py:24
  25.6 10.4 %collective-permute-start.16 = (f32[4,1,16]{2,1,0:T(1,128)S(1)}, f32[4,1,16]{2,1,0:T(1,128)S(1)}, u32[]{:S(2)}, u32[]{:S(2)}) collective-permute-start(f32[4,1,16]{2,1,0:T(1,128)S(1)} %get-tuple-element.92), channel_id=1, source_target_pairs={{8,0},{16,8},{24,16},{32,24},{40,32},{48,40},{56,48},{64,56},{72,6... | collective-permute-start | bytes 776 | tf_op jit(solution)/shard_map/ppermute | solution.py:25
  32.9 8.5 %collective-permute-start.17 = (f32[4,1,16]{2,1,0:T(1,128)S(1)}, f32[4,1,16]{2,1,0:T(1,128)S(1)}, u32[]{:S(2)}, u32[]{:S(2)}) collective-permute-start(f32[4,1,16]{2,1,0:T(1,128)S(1)} %get-tuple-element.91), channel_id=1, source_target_pairs={{0,8},{8,16},{16,24},{24,32},{32,40},{40,48},{48,56},{56,64},{64,7... | collective-permute-start | bytes 776 | tf_op jit(solution)/shard_map/ppermute | solution.py:24
  42.7 13.0 %collective-permute-start.3 = (f32[2,32,26,1]{1,0,3,2:T(2,128)S(1)}, f32[2,32,26,1]{1,0,3,2:T(2,128)S(1)}, u32[]{:S(2)}, u32[]{:S(2)}) collective-permute-start(f32[2,32,26,1]{1,0,3,2:T(2,128)S(1)} %copy.5), channel_id=1, source_target_pairs={{1,0},{2,1},{3,2},{4,3},{5,4},{6,5},{7,6},{0,7},{9,8},{10,9},{11,1... | collective-permute-start | bytes 19976 | tf_op jit(solution)/shard_map/ppermute | solution.py:25
  45.7 10.9 %collective-permute-start.2 = (f32[2,32,26,1]{1,0,3,2:T(2,128)S(1)}, f32[2,32,26,1]{1,0,3,2:T(2,128)S(1)}, u32[]{:S(2)}, u32[]{:S(2)}) collective-permute-start(f32[2,32,26,1]{1,0,3,2:T(2,128)S(1)} %copy.4), channel_id=1, source_target_pairs={{0,1},{1,2},{2,3},{3,4},{4,5},{5,6},{6,7},{7,0},{8,9},{9,10},{10,1... | collective-permute-start | bytes 19976 | tf_op jit(solution)/shard_map/ppermute | solution.py:24
  49.8 19.4 %collective-permute-start.18 = (f32[4,5,1]{2,1,0:T(8,128)}, f32[4,5,1]{2,1,0:T(8,128)}, u32[]{:S(2)}, u32[]{:S(2)}) collective-permute-start(f32[4,5,1]{2,1,0:T(8,128)} %get-tuple-element.68), channel_id=1, source_target_pairs={{1,0},{2,1},{3,2},{4,3},{5,4},{6,5},{7,6},{0,7},{9,8},{10,9},{11,1... | collective-permute-start | bytes 248 | tf_op jit(solution)/shard_map/ppermute | solution.py:25
  53.1 16.1 %collective-permute-start.19 = (f32[4,5,1]{2,1,0:T(8,128)}, f32[4,5,1]{2,1,0:T(8,128)}, u32[]{:S(2)}, u32[]{:S(2)}) collective-permute-start(f32[4,5,1]{2,1,0:T(8,128)} %get-tuple-element.67), channel_id=1, source_target_pairs={{0,1},{1,2},{2,3},{3,4},{4,5},{5,6},{6,7},{7,0},{8,9},{9,10},{10,1... | collective-permute-start | bytes 248 | tf_op jit(solution)/shard_map/ppermute | solution.py:24
  71.7 13.0 %collective-permute-start.20 = (f32[4,1,16]{2,1,0:T(1,128)S(1)}, f32[4,1,16]{2,1,0:T(1,128)S(1)}, u32[]{:S(2)}, u32[]{:S(2)}) collective-permute-start(f32[4,1,16]{2,1,0:T(1,128)S(1)} %get-tuple-element.86), channel_id=1, source_target_pairs={{8,0},{16,8},{24,16},{32,24},{40,32},{48,40},{56,48},{64,56},{72,6... | collective-permute-start | bytes 776 | tf_op jit(solution)/shard_map/ppermute | solution.py:25
  73.7 11.1 %collective-permute-start.21 = (f32[4,1,16]{2,1,0:T(1,128)S(1)}, f32[4,1,16]{2,1,0:T(1,128)S(1)}, u32[]{:S(2)}, u32[]{:S(2)}) collective-permute-start(f32[4,1,16]{2,1,0:T(1,128)S(1)} %get-tuple-element.85), channel_id=1, source_target_pairs={{0,8},{8,16},{16,24},{24,32},{32,40},{40,48},{48,56},{56,64},{64,7... | collective-permute-start | bytes 776 | tf_op jit(solution)/shard_map/ppermute | solution.py:24
  76.1 60.6 %collective-permute-start.4 = (f32[32,1,128]{2,1,0:T(1,128)S(1)}, f32[32,1,128]{2,1,0:T(1,128)S(1)}, u32[]{:S(2)}, u32[]{:S(2)}) collective-permute-start(f32[32,1,128]{2,1,0:T(1,128)S(1)} %get-tuple-element.60), channel_id=1, source_target_pairs={{8,0},{16,8},{24,16},{32,24},{40,32},{48,40},{56,48},{64,56},{72,6... | collective-permute-start | bytes 49160 | tf_op jit(solution)/shard_map/ppermute | solution.py:25
  82.8 53.9 %collective-permute-start.5 = (f32[32,1,128]{2,1,0:T(1,128)S(1)}, f32[32,1,128]{2,1,0:T(1,128)S(1)}, u32[]{:S(2)}, u32[]{:S(2)}) collective-permute-start(f32[32,1,128]{2,1,0:T(1,128)S(1)} %get-tuple-element.59), channel_id=1, source_target_pairs={{0,8},{8,16},{16,24},{24,32},{32,40},{40,48},{48,56},{56,64},{64,7... | collective-permute-start | bytes 49160 | tf_op jit(solution)/shard_map/ppermute | solution.py:24
  84.9 6.8 %collective-permute-start.23 = (f32[4,5,1]{2,1,0:T(8,128)S(1)}, f32[4,5,1]{2,1,0:T(8,128)S(1)}, u32[]{:S(2)}, u32[]{:S(2)}) collective-permute-start(f32[4,5,1]{2,1,0:T(8,128)S(1)} %get-tuple-element.66), channel_id=1, source_target_pairs={{0,1},{1,2},{2,3},{3,4},{4,5},{5,6},{6,7},{7,0},{8,9},{9,10},{10,1... | collective-permute-start | bytes 248 | tf_op jit(solution)/shard_map/ppermute | solution.py:24
  89.2 5.6 %collective-permute-start.22 = (f32[4,5,1]{2,1,0:T(8,128)S(1)}, f32[4,5,1]{2,1,0:T(8,128)S(1)}, u32[]{:S(2)}, u32[]{:S(2)}) collective-permute-start(f32[4,5,1]{2,1,0:T(8,128)S(1)} %get-tuple-element.65), channel_id=1, source_target_pairs={{1,0},{2,1},{3,2},{4,3},{5,4},{6,5},{7,6},{0,7},{9,8},{10,9},{11,1... | collective-permute-start | bytes 248 | tf_op jit(solution)/shard_map/ppermute | solution.py:25
  95.6 8.4 %collective-permute-start.24 = (f32[4,1,16]{2,1,0:T(1,128)S(1)}, f32[4,1,16]{2,1,0:T(1,128)S(1)}, u32[]{:S(2)}, u32[]{:S(2)}) collective-permute-start(f32[4,1,16]{2,1,0:T(1,128)S(1)} %get-tuple-element.80), channel_id=1, source_target_pairs={{8,0},{16,8},{24,16},{32,24},{40,32},{48,40},{56,48},{64,56},{72,6... | collective-permute-start | bytes 776 | tf_op jit(solution)/shard_map/ppermute | solution.py:25
  102.1 8.5 %collective-permute-start.25 = (f32[4,1,16]{2,1,0:T(1,128)S(1)}, f32[4,1,16]{2,1,0:T(1,128)S(1)}, u32[]{:S(2)}, u32[]{:S(2)}) collective-permute-start(f32[4,1,16]{2,1,0:T(1,128)S(1)} %get-tuple-element.79), channel_id=1, source_target_pairs={{0,8},{8,16},{16,24},{24,32},{32,40},{40,48},{48,56},{56,64},{64,7... | collective-permute-start | bytes 776 | tf_op jit(solution)/shard_map/ppermute | solution.py:24
  110.7 6.8 %collective-permute-start.27 = (f32[4,5,1]{2,1,0:T(8,128)S(1)}, f32[4,5,1]{2,1,0:T(8,128)S(1)}, u32[]{:S(2)}, u32[]{:S(2)}) collective-permute-start(f32[4,5,1]{2,1,0:T(8,128)S(1)} %get-tuple-element.64), channel_id=1, source_target_pairs={{0,1},{1,2},{2,3},{3,4},{4,5},{5,6},{6,7},{7,0},{8,9},{9,10},{10,1... | collective-permute-start | bytes 248 | tf_op jit(solution)/shard_map/ppermute | solution.py:24
  113.3 6.0 %collective-permute-start.26 = (f32[4,5,1]{2,1,0:T(8,128)S(1)}, f32[4,5,1]{2,1,0:T(8,128)S(1)}, u32[]{:S(2)}, u32[]{:S(2)}) collective-permute-start(f32[4,5,1]{2,1,0:T(8,128)S(1)} %get-tuple-element.63), channel_id=1, source_target_pairs={{1,0},{2,1},{3,2},{4,3},{5,4},{6,5},{7,6},{0,7},{9,8},{10,9},{11,1... | collective-permute-start | bytes 248 | tf_op jit(solution)/shard_map/ppermute | solution.py:25
  119.4 4.4 %collective-permute-start.28 = (f32[4,1,16]{2,1,0:T(1,128)S(1)}, f32[4,1,16]{2,1,0:T(1,128)S(1)}, u32[]{:S(2)}, u32[]{:S(2)}) collective-permute-start(f32[4,1,16]{2,1,0:T(1,128)S(1)} %get-tuple-element.74), channel_id=1, source_target_pairs={{8,0},{16,8},{24,16},{32,24},{40,32},{48,40},{56,48},{64,56},{72,6... | collective-permute-start | bytes 776 | tf_op jit(solution)/shard_map/ppermute | solution.py:25
  121.3 8.5 %collective-permute-start.29 = (f32[4,1,16]{2,1,0:T(1,128)S(1)}, f32[4,1,16]{2,1,0:T(1,128)S(1)}, u32[]{:S(2)}, u32[]{:S(2)}) collective-permute-start(f32[4,1,16]{2,1,0:T(1,128)S(1)} %get-tuple-element.73), channel_id=1, source_target_pairs={{0,8},{8,16},{16,24},{24,32},{32,40},{40,48},{48,56},{56,64},{64,7... | collective-permute-start | bytes 776 | tf_op jit(solution)/shard_map/ppermute | solution.py:24
  129.9 16.3 %collective-permute-start.31 = (f32[4,5,1]{2,1,0:T(8,128)S(1)}, f32[4,5,1]{2,1,0:T(8,128)S(1)}, u32[]{:S(2)}, u32[]{:S(2)}) collective-permute-start(f32[4,5,1]{2,1,0:T(8,128)S(1)} %get-tuple-element.62), channel_id=1, source_target_pairs={{0,1},{1,2},{2,3},{3,4},{4,5},{5,6},{6,7},{7,0},{8,9},{9,10},{10,1... | collective-permute-start | bytes 248 | tf_op jit(solution)/shard_map/ppermute | solution.py:24
  134.7 11.4 %collective-permute-start.30 = (f32[4,5,1]{2,1,0:T(8,128)S(1)}, f32[4,5,1]{2,1,0:T(8,128)S(1)}, u32[]{:S(2)}, u32[]{:S(2)}) collective-permute-start(f32[4,5,1]{2,1,0:T(8,128)S(1)} %get-tuple-element.61), channel_id=1, source_target_pairs={{1,0},{2,1},{3,2},{4,3},{5,4},{6,5},{7,6},{0,7},{9,8},{10,9},{11,1... | collective-permute-start | bytes 248 | tf_op jit(solution)/shard_map/ppermute | solution.py:25
  139.2 17.9 %collective-permute-start.7 = (f32[32,26,1]{2,1,0:T(8,128)}, f32[32,26,1]{2,1,0:T(8,128)}, u32[]{:S(2)}, u32[]{:S(2)}) collective-permute-start(f32[32,26,1]{2,1,0:T(8,128)} %get-tuple-element.42), channel_id=1, source_target_pairs={{0,1},{1,2},{2,3},{3,4},{4,5},{5,6},{6,7},{7,0},{8,9},{9,10},{10,1... | collective-permute-start | bytes 9992 | tf_op jit(solution)/shard_map/ppermute | solution.py:24
  143.3 21.2 %collective-permute-start.6 = (f32[32,26,1]{2,1,0:T(8,128)}, f32[32,26,1]{2,1,0:T(8,128)}, u32[]{:S(2)}, u32[]{:S(2)}) collective-permute-start(f32[32,26,1]{2,1,0:T(8,128)} %get-tuple-element.41), channel_id=1, source_target_pairs={{1,0},{2,1},{3,2},{4,3},{5,4},{6,5},{7,6},{0,7},{9,8},{10,9},{11,1... | collective-permute-start | bytes 9992 | tf_op jit(solution)/shard_map/ppermute | solution.py:25
  166.7 4.4 %collective-permute-start.8 = (f32[32,1,128]{2,1,0:T(1,128)S(1)}, f32[32,1,128]{2,1,0:T(1,128)S(1)}, u32[]{:S(2)}, u32[]{:S(2)}) collective-permute-start(f32[32,1,128]{2,1,0:T(1,128)S(1)} %get-tuple-element.54), channel_id=1, source_target_pairs={{8,0},{16,8},{24,16},{32,24},{40,32},{48,40},{56,48},{64,56},{72,6... | collective-permute-start | bytes 49160 | tf_op jit(solution)/shard_map/ppermute | solution.py:25
  168.6 8.8 %collective-permute-start.9 = (f32[32,1,128]{2,1,0:T(1,128)S(1)}, f32[32,1,128]{2,1,0:T(1,128)S(1)}, u32[]{:S(2)}, u32[]{:S(2)}) collective-permute-start(f32[32,1,128]{2,1,0:T(1,128)S(1)} %get-tuple-element.53), channel_id=1, source_target_pairs={{0,8},{8,16},{16,24},{24,32},{32,40},{40,48},{48,56},{56,64},{64,7... | collective-permute-start | bytes 49160 | tf_op jit(solution)/shard_map/ppermute | solution.py:24
  177.7 17.0 %collective-permute-start.11 = (f32[32,26,1]{2,1,0:T(8,128)S(1)}, f32[32,26,1]{2,1,0:T(8,128)S(1)}, u32[]{:S(2)}, u32[]{:S(2)}) collective-permute-start(f32[32,26,1]{2,1,0:T(8,128)S(1)} %get-tuple-element.40), channel_id=1, source_target_pairs={{0,1},{1,2},{2,3},{3,4},{4,5},{5,6},{6,7},{7,0},{8,9},{9,10},{10,1... | collective-permute-start | bytes 9992 | tf_op jit(solution)/shard_map/ppermute | solution.py:24
  181.4 20.0 %collective-permute-start.10 = (f32[32,26,1]{2,1,0:T(8,128)S(1)}, f32[32,26,1]{2,1,0:T(8,128)S(1)}, u32[]{:S(2)}, u32[]{:S(2)}) collective-permute-start(f32[32,26,1]{2,1,0:T(8,128)S(1)} %get-tuple-element.39), channel_id=1, source_target_pairs={{1,0},{2,1},{3,2},{4,3},{5,4},{6,5},{7,6},{0,7},{9,8},{10,9},{11,1... | collective-permute-start | bytes 9992 | tf_op jit(solution)/shard_map/ppermute | solution.py:25
  202.2 4.6 %collective-permute-start.12 = (f32[32,1,128]{2,1,0:T(1,128)S(1)}, f32[32,1,128]{2,1,0:T(1,128)S(1)}, u32[]{:S(2)}, u32[]{:S(2)}) collective-permute-start(f32[32,1,128]{2,1,0:T(1,128)S(1)} %get-tuple-element.48), channel_id=1, source_target_pairs={{8,0},{16,8},{24,16},{32,24},{40,32},{48,40},{56,48},{64,56},{72,6... | collective-permute-start | bytes 49160 | tf_op jit(solution)/shard_map/ppermute | solution.py:25
  204.1 8.9 %collective-permute-start.13 = (f32[32,1,128]{2,1,0:T(1,128)S(1)}, f32[32,1,128]{2,1,0:T(1,128)S(1)}, u32[]{:S(2)}, u32[]{:S(2)}) collective-permute-start(f32[32,1,128]{2,1,0:T(1,128)S(1)} %get-tuple-element.47), channel_id=1, source_target_pairs={{0,8},{8,16},{16,24},{24,32},{32,40},{40,48},{48,56},{56,64},{64,7... | collective-permute-start | bytes 49160 | tf_op jit(solution)/shard_map/ppermute | solution.py:24
  213.3 17.0 %collective-permute-start.15 = (f32[32,26,1]{2,1,0:T(8,128)S(1)}, f32[32,26,1]{2,1,0:T(8,128)S(1)}, u32[]{:S(2)}, u32[]{:S(2)}) collective-permute-start(f32[32,26,1]{2,1,0:T(8,128)S(1)} %get-tuple-element.38), channel_id=1, source_target_pairs={{0,1},{1,2},{2,3},{3,4},{4,5},{5,6},{6,7},{7,0},{8,9},{9,10},{10,1... | collective-permute-start | bytes 9992 | tf_op jit(solution)/shard_map/ppermute | solution.py:24
  217.0 20.0 %collective-permute-start.14 = (f32[32,26,1]{2,1,0:T(8,128)S(1)}, f32[32,26,1]{2,1,0:T(8,128)S(1)}, u32[]{:S(2)}, u32[]{:S(2)}) collective-permute-start(f32[32,26,1]{2,1,0:T(8,128)S(1)} %get-tuple-element.37), channel_id=1, source_target_pairs={{1,0},{2,1},{3,2},{4,3},{5,4},{6,5},{7,6},{0,7},{9,8},{10,9},{11,1... | collective-permute-start | bytes 9992 | tf_op jit(solution)/shard_map/ppermute | solution.py:25
  (13 other events, 244.9 us)
where the time goes:
time: 240 us; the launch traced here: 239 us
  starting transfers between devices  111 us (46%)
  waiting for transfers between devices  78.6 us (33%)
  local copies, waits for them, and re-layouts  31.2 us (13%)
  other arithmetic  16.8 us (7%)
    ppermute x16, starting transfers between devices, extended(): after = lax.ppermute(first, axis, down)  64.5 us
    ppermute x16, waiting for transfers between devices, extended(): before = lax.ppermute(last, axis, up)  52.8 us
    ppermute x16, starting transfers between devices, extended(): before = lax.ppermute(last, axis, up)  46.6 us
    ppermute x16, waiting for transfers between devices, extended(): after = lax.ppermute(first, axis, down)  25.8 us
    reshape x2, local copies, waits for them, and re-layouts, restrict(): values.reshape(depth // COARSEN, COARSEN, width_x // COARSEN, COARSEN, wi...  10.8 us
    reduce_sum x2, other arithmetic, restrict(): return jnp.mean(blocks, axis=(1, 3, 5))  6.64 us
    reshape x1, local copies, waits for them, and re-layouts, prolong(): return spread.reshape(depth * COARSEN, width_x * COARSEN, width_y * COARSEN)  5.89 us
  transfers between devices with their start and end apart: 32, of which 13 were waited for; matrix products, arithmetic and copies ran while one was open for 15% of the time, Pallas kernels for 0%

commit v1 on v0

v1 whole, which is shorter than its diff:
```python
import functools

import jax
import jax.numpy as jnp
from jax import lax
from jax.experimental import pallas as pl
from jax.experimental.pallas import tpu as pltpu
from jax.sharding import PartitionSpec as P

SWEEPS = 3
COARSE_SWEEPS = 4
COARSEN = 8
SHIFT = 0.1
LMIN = 0.3
LMAX = 2.0
OMEGA = 0.8

MESH = pl.DeviceIdType.MESH
NZ, NX, NY = 32, 24, 128
RIM = 4
ROWS = NX + 2 * RIM
NZC, NXC, NYC = NZ // COARSEN, NX // COARSEN, NY // COARSEN
F32 = jnp.float32
NEIGHBOURS = ((1, 0), (-1, 0), (0, 1), (0, -1), (1, 1), (1, -1), (-1, 1), (-1, -1))


def lanes(x, s):
    return pltpu.roll(x, s % x.shape[1], 1)


def rows(x, s):
    return pltpu.roll(x, s % x.shape[0], 0)


def iota(shape, dim):
    return lax.broadcasted_iota(jnp.int32, shape, dim)


def coefficients():
    theta = (LMAX + LMIN) / 2.0
    delta = (LMAX - LMIN) / 2.0
    sigma = theta / delta
    rho = 1.0 / sigma
    steps = []
    for _ in range(SWEEPS):
        after = 1.0 / (2.0 * sigma - rho)
        steps.append((after * rho, 2.0 * after / delta))
        rho = after
    return theta, steps


def kernel(sizes, v_hbm, s_hbm, c_hbm, o_ref, V, C, S, W, RT, D, U, K, KW, KR, KD, EO, PR, MR, ME, CS, CR, XS, XR,
           own_sem, fs, fr, ks, kr, cs, cr, xs, xr):
    ngx, ngy = sizes
    gx, gy = lax.axis_index("gx"), lax.axis_index("gy")

    def at(d):
        return (lax.rem(gx + d[0] + ngx, ngx), lax.rem(gy + d[1] + ngy, ngy))

    barrier = pltpu.get_barrier_semaphore()
    for d in NEIGHBOURS:
        pl.semaphore_signal(barrier, inc=1, device_id=at(d), device_id_type=MESH)
    loads = []
    for i, (src, dst) in enumerate(((v_hbm, V), (c_hbm, C), (s_hbm, S))):
        loads.append(pltpu.make_async_copy(src, dst.at[:, 0:NX, :], own_sem.at[i]))
        loads[-1].start()

    theta, steps = coefficients()
    lane24 = iota((NX, NY), 1)
    lane32 = iota((ROWS, NY), 1)
    lane8 = iota((8, NY), 1)
    row8 = iota((8, NY), 0)

    for zc in range(NZC):
        a, b = iota((NY, NY), 0), iota((NY, NY), 1)
        MR[zc] = jnp.where(b == zc * 32 + 8 + a // COARSEN, 1.0 / COARSEN**3, 0.0).astype(F32)
        ME[zc] = jnp.where(a == zc * 32 + 8 + b // COARSEN, 1.0, 0.0).astype(F32)

    def three_rows(x):
        out = jnp.zeros((8, NY), F32)
        for j in range(NXC):
            out = jnp.where(row8 == j, jnp.sum(x[8 * j : 8 * j + 8], axis=0, keepdims=True), out)
        return out

    def tile_of(sums):
        out = jnp.zeros((8, NY), F32)
        for zc in range(NZC):
            out = out + jnp.dot(three_rows(sums[zc]), MR[zc], precision=lax.Precision.HIGHEST, preferred_element_type=F32)
        return out

    def extract(f, ref):
        def step(m, accs):
            new = []
            for k in range(4):
                z = 4 * m + k
                turned = pltpu.roll(ref[z, 0:NX], 4 * z, 1)
                window = lax.shift_right_logical((lane24 + (8 - 4 * k + NY)) & (NY - 1), 4) == m
                new.append(jnp.where(window, turned, accs[k]))
            return tuple(new)

        accs = lax.fori_loop(0, 8, step, tuple(jnp.zeros((NX, NY), F32) for _ in range(4)))
        phase = lax.shift_right_logical(lane24, 2)

        def pick(j):
            out = accs[0]
            for k in range(1, 4):
                out = jnp.where(((phase + j) & 3) == k, accs[k], out)
            return out

        K[f, 1, 0:NX] = pick(0)
        K[f, 2, 0:NX] = lanes(pick(3), -4)
        K[f, 4, 0:NX] = lanes(pick(1), 4)
        K[f, 3, 0:NX] = lanes(pick(2), 8)

    for i, ref in enumerate((V, C, S)):
        loads[i].wait()
        extract(i, ref)
    csums = []
    for zc in range(NZC):
        csums.append(lax.fori_loop(1, COARSEN, lambda i, a, zc=zc: a + C[zc * COARSEN + i, 0:NX], C[zc * COARSEN, 0:NX]))
    CS[...] = tile_of(csums)

    pl.semaphore_wait(barrier, len(NEIGHBOURS))

    def send(src, dst, send_sem, recv_sem, d):
        copy = pltpu.make_async_remote_copy(
            src_ref=src, dst_ref=dst, send_sem=send_sem, recv_sem=recv_sem, device_id=at(d), device_id_type=MESH
        )
        copy.start()
        return copy

    low, high = slice(NX, NX + RIM), slice(NX + RIM, ROWS)
    first, last = slice(0, RIM), slice(NX - RIM, NX)
    diag_copies = [
        send(K.at[:, 4, last], K.at[:, 0, high], ks.at[4], kr.at[4], (1, 1)),
        send(K.at[:, 1, last], K.at[:, 5, high], ks.at[5], kr.at[5], (1, -1)),
        send(K.at[:, 4, first], K.at[:, 0, low], ks.at[6], kr.at[6], (-1, 1)),
        send(K.at[:, 1, first], K.at[:, 5, low], ks.at[7], kr.at[7], (-1, -1)),
    ]
    near_copies = []
    for i, (src, dst) in enumerate(((v_hbm, V), (c_hbm, C), (s_hbm, S))):
        near_copies.append(send(src.at[:, last, :], dst.at[:, high, :], fs.at[2 * i], fr.at[2 * i], (1, 0)))
        near_copies.append(send(src.at[:, first, :], dst.at[:, low, :], fs.at[2 * i + 1], fr.at[2 * i + 1], (-1, 0)))
    side_copies = [
        send(K.at[:, 1:5, last], K.at[:, 1:5, high], ks.at[0], kr.at[0], (1, 0)),
        send(K.at[:, 1:5, first], K.at[:, 1:5, low], ks.at[1], kr.at[1], (-1, 0)),
    ]
    strip_copies = [
        send(K.at[:, 4, 0:NX], K.at[:, 0, 0:NX], ks.at[2], kr.at[2], (0, 1)),
        send(K.at[:, 1, 0:NX], K.at[:, 5, 0:NX], ks.at[3], kr.at[3], (0, -1)),
    ]
    cond_copies = [send(CS, CR.at[i], cs.at[i], cr.at[i], d) for i, d in enumerate(NEIGHBOURS)]


    for copy in near_copies:
        copy.wait_recv()
    not_last = lane32 != NY - 1
    not_first = lane32 != 0

    def setup(z, acc):
        up, dn = (z + 1) & (NZ - 1), (z + NZ - 1) & (NZ - 1)
        c, v = C[z], V[z]
        ws = [
            c + C[up],
            c + C[dn],
            c + rows(c, -1),
            c + rows(c, 1),
            jnp.where(not_last, c + lanes(c, -1), 0.0),
            jnp.where(not_first, c + lanes(c, 1), 0.0),
        ]
        vs = [V[up], V[dn], rows(v, -1), rows(v, 1), lanes(v, -1), lanes(v, 1)]
        total = ((ws[0] + ws[1]) + (ws[2] + ws[3])) + (ws[4] + ws[5])
        flow = ((ws[0] * vs[0] + ws[1] * vs[1]) + (ws[2] * vs[2] + ws[3] * vs[3])) + (ws[4] * vs[4] + ws[5] * vs[5])
        diag = SHIFT + 0.5 * total
        residual = (S[z] - diag * v) + 0.5 * flow
        inv = 1.0 / diag
        half = 0.5 * inv
        for i in range(6):
            W[i, z] = ws[i] * half
        rt = residual * inv
        RT[z] = rt
        D[0, z] = rt * (1.0 / theta)
        return acc + residual[0:NX]

    rsums = []
    for zc in range(NZC):
        rsums.append(lax.fori_loop(zc * COARSEN, (zc + 1) * COARSEN, setup, jnp.zeros((NX, NY), F32)))

    for copy in strip_copies + cond_copies[:4]:
        copy.wait_recv()
    col0 = (lane24 & 3) == 0

    def face(outer, inner, turn_outer, turn_inner):
        vo, vi, co, ci = K[0, outer, 0:NX], K[0, inner, 0:NX], K[1, outer, 0:NX], K[1, inner, 0:NX]
        if turn_outer:
            vo, co = lanes(vo, turn_outer), lanes(co, turn_outer)
        if turn_inner:
            vi, ci = lanes(vi, turn_inner), lanes(ci, turn_inner)
        flux = jnp.where(col0, 0.5 * (co + ci) * (vo - vi), 0.0)
        for s in (4, 8, 16):
            flux = flux + lanes(flux, -s)
        return three_rows(flux) * (1.0 / COARSEN**3)

    rhs = tile_of(rsums)
    rhs = rhs + jnp.where((lane8 & 31) == 8, lanes(face(0, 1, -3, 0), 8), 0.0)
    rhs = rhs + jnp.where((lane8 & 31) == 23, lanes(face(5, 4, 0, -3), 23), 0.0)

    spot = lane8 & 31

    def widen(left, centre, right):
        out = jnp.where((spot >= 8) & (spot < 24), centre, 0.0)
        if left is not None:
            out = jnp.where((spot >= 4) & (spot < 8), lanes(left, -16), out)
            out = jnp.where((spot >= 24) & (spot < 28), lanes(right, 16), out)
        return out

    def stack(below, centre, above):
        top = jnp.where(row8 < 3, centre, jnp.where(row8 < 6, rows(above, 3), 0.0))
        bottom = jnp.where(row8 >= 5, rows(below, 5), 0.0)
        return jnp.concatenate([top, bottom], axis=0)

    def coarse_weights(c):
        c = c * (0.5 / COARSEN**2)
        ws = [c + lanes(c, 32), c + lanes(c, -32), c + rows(c, -1), c + rows(c, 1), c + lanes(c, -1), c + lanes(c, 1)]
        diag = SHIFT + (((ws[0] + ws[1]) + (ws[2] + ws[3])) + (ws[4] + ws[5]))
        inv = OMEGA / diag
        return inv, ws

    own = CS[...]
    inv, _ = coarse_weights(stack(CR[0], widen(CR[2], own, CR[3]), CR[1]))
    XS[...] = rhs * inv[0:8]
    start_copies = [send(XS, XR.at[i], xs.at[i], xr.at[i], d) for i, d in enumerate(NEIGHBOURS)]

    def image(z, d):
        up, dn = (z + 1) & (NZ - 1), (z + NZ - 1) & (NZ - 1)
        c = D[d, z]
        near = [D[d, up], D[d, dn], rows(c, -1), rows(c, 1), lanes(c, -1), lanes(c, 1)]
        terms = [W[i, z] * near[i] for i in range(6)]
        return c, ((terms[0] + terms[1]) + (terms[2] + terms[3])) + (terms[4] + terms[5])

    def sweep_one(z, carry):
        c, gain = image(z, 0)
        rt = (RT[z] - c) + gain
        RT[z] = rt
        D[1, z] = steps[0][0] * c + steps[0][1] * rt
        return carry

    def sweep_two(z, carry):
        c, gain = image(z, 1)
        rt = (RT[z] - c) + gain
        RT[z] = rt
        d = steps[1][0] * c + steps[1][1] * rt
        D[2, z] = d
        U[z] = D[0, z, 0:NX] + c[0:NX] + d[0:NX]
        return carry

    lax.fori_loop(0, NZ, sweep_one, 0)
    lax.fori_loop(0, NZ, sweep_two, 0)

    for copy in side_copies + diag_copies:
        copy.wait_recv()
    column = lane32 & 3
    ends, starts = column == 3, column == 0

    def strip_near(ref_of, g):
        x = ref_of(g)
        after, before = lanes(x, -1), lanes(x, 1)
        if g not in (2, 5):
            after = jnp.where(ends, lanes(ref_of(g + 1), 3), after)
        if g not in (0, 3):
            before = jnp.where(starts, lanes(ref_of(g - 1), -3), before)
        return x, [lanes(x, -4), lanes(x, 4), rows(x, -1), rows(x, 1), after, before]

    for g in range(6):
        c, cs_ = strip_near(lambda i: K[1, i], g)
        v, vs = strip_near(lambda i: K[0, i], g)
        ws = [c + n for n in cs_]
        total = ((ws[0] + ws[1]) + (ws[2] + ws[3])) + (ws[4] + ws[5])
        flow = ws[0] * vs[0]
        for i in range(1, 6):
            flow = flow + ws[i] * vs[i]
        diag = SHIFT + 0.5 * total
        inv = 1.0 / diag
        half = 0.5 * inv
        for i in range(6):
            KW[i, g] = ws[i] * half
        rt = ((K[2, g] - diag * v) + 0.5 * flow) * inv
        KR[g] = rt
        KD[0, g] = rt * (1.0 / theta)
    for k in range(SWEEPS):
        for g in range(6) if k < SWEEPS - 1 else (1, 4):
            c, near = strip_near(lambda i: KD[k, i], g)
            rt = KR[g] - c
            for i in range(6):
                rt = rt + KW[i, g] * near[i]
            KR[g] = rt
            KD[k + 1, g] = steps[k][0] * c + steps[k][1] * rt
    left = ((KD[0, 1] + KD[1, 1]) + (KD[2, 1] + KD[3, 1]))[0:NX]
    right = ((KD[0, 4] + KD[1, 4]) + (KD[2, 4] + KD[3, 4]))[0:NX]
    left = lanes(left, 4)
    even = (lane24 & 7) < 4
    EO[0] = jnp.where(even, right, left)
    EO[1] = jnp.where(even, left, right)

    for copy in cond_copies[4:] + start_copies:
        copy.wait_recv()

    def extended(ref, own):
        return stack(
            widen(ref[4], ref[0], ref[5]), widen(ref[2], own, ref[3]), widen(ref[6], ref[1], ref[7])
        )

    inv, ws = coarse_weights(extended(CR, own))
    ws = [w * inv for w in ws]
    start = extended(XR, XS[...])
    x = start
    for _ in range(COARSE_SWEEPS - 1):
        near = [lanes(x, 32), lanes(x, -32), rows(x, -1), rows(x, 1), lanes(x, -1), lanes(x, 1)]
        terms = [ws[i] * near[i] for i in range(6)]
        gain = ((terms[0] + terms[1]) + (terms[2] + terms[3])) + (terms[4] + terms[5])
        x = (start + (1.0 - OMEGA) * x) + gain
    x = x[0:8]
    for zc in range(NZC):
        spread = jnp.dot(x, ME[zc], precision=lax.Precision.HIGHEST, preferred_element_type=F32)
        for j in range(NXC):
            PR[zc, 8 * j : 8 * j + 8] = jnp.broadcast_to(spread[j : j + 1], (8, NY))

    edge = (lane24 < 4) | (lane24 >= NY - 4)

    def finish(z, carry):
        c, gain = image(z, 2)
        rt = (RT[z] - c) + gain
        d = steps[2][0] * c + steps[2][1] * rt
        total = U[z] + d[0:NX]
        strip = pltpu.roll(EO[z & 1], (2 * NY - 4 - 4 * z) & (NY - 1), 1)
        total = jnp.where(edge, strip, total)
        o_ref[z] = (V[z, 0:NX] + total) + PR[z // COARSEN]
        return carry

    lax.fori_loop(0, NZ, finish, 0)
    for copy in near_copies + side_copies + strip_copies + diag_copies + cond_copies + start_copies:
        copy.wait_send()


def solution(mesh):
    sizes = (mesh.shape["gx"], mesh.shape["gy"])

    def body(iterate, source, conduct):
        plane = (NZ, ROWS, NY)
        dma = pltpu.SemaphoreType.DMA
        return pl.pallas_call(
            functools.partial(kernel, sizes),
            out_shape=jax.ShapeDtypeStruct((NZ, NX, NY), F32),
            in_specs=[pl.BlockSpec(memory_space=pl.ANY)] * 3,
            out_specs=pl.BlockSpec(memory_space=pltpu.VMEM),
            scratch_shapes=[
                pltpu.VMEM(plane, F32),
                pltpu.VMEM(plane, F32),
                pltpu.VMEM(plane, F32),
                pltpu.VMEM((6,) + plane, F32),
                pltpu.VMEM(plane, F32),
                pltpu.VMEM((3,) + plane, F32),
                pltpu.VMEM((NZ, NX, NY), F32),
                pltpu.VMEM((3, 6, ROWS, NY), F32),
                pltpu.VMEM((6, 6, ROWS, NY), F32),
                pltpu.VMEM((6, ROWS, NY), F32),
                pltpu.VMEM((4, 6, ROWS, NY), F32),
                pltpu.VMEM((2, NX, NY), F32),
                pltpu.VMEM((NZC, NX, NY), F32),
                pltpu.VMEM((NZC, NY, NY), F32),
                pltpu.VMEM((NZC, NY, NY), F32),
                pltpu.VMEM((8, NY), F32),
                pltpu.VMEM((8, 8, NY), F32),
                pltpu.VMEM((8, NY), F32),
                pltpu.VMEM((8, 8, NY), F32),
                dma((3,)),
                dma((6,)),
                dma((6,)),
                dma((8,)),
                dma((8,)),
                dma((8,)),
                dma((8,)),
                dma((8,)),
                dma((8,)),
            ],
            compiler_params=pltpu.CompilerParams(collective_id=0, has_side_effects=True),
        )(iterate, source, conduct)

    return jax.shard_map(
        body,
        mesh=mesh,
        in_specs=(P(None, "gx", "gy"), P(None, "gx", "gy"), P(None, "gx", "gy")),
        out_specs=P(None, "gx", "gy"),
        check_vma=False,
    )
```

time: 240 us -> 35.7 us (0.15)
  the two profiles are of different devices: /device:TPU:8 before, /device:TPU:1 now
where the time goes in v1:
time: 35.7 us; the launch traced here: 35.5 us
  Pallas kernels  33.7 us (94%)
  local copies, waits for them, and re-layouts  1.77 us (5%)
    pallas_call x1, Pallas kernels, body(): pl.pallas_call(functools.partial(kernel, sizes), out_shape=jax.ShapeDtype...  33.7 us
    unnamed x1, local copies, waits for them, and re-layouts  1.77 us

profile of v1, /device:TPU:1, one launch (start us, length us, event | category | flops | bytes accessed | tf_op | source)
XLA Modules:
  0.0 35.5 jit_solution(8504940532242286366)
XLA Ops:
  0.0 33.7 %shard_map.37 = f32[32,24,128]{2,1,0:T(8,128)} custom-call(f32[32,24,128]{2,1,0:T(8,128)} %v_hbm.1, f32[32,24,128]{2,1,0:T(8,128)} %s_hbm.1, f32[32,24,128]{2,1,0:T(8,128)} %c_hbm.1), custom_call_target="tpu_custom_call" | custom-call | tf_op jit(solution)/shard_map/pallas_call | solution.py:351
  33.7 1.8 %copy.5 = f32[32,24,128]{2,1,0:T(8,128)} copy(f32[32,24,128]{2,1,0:T(8,128)} %shard_map.37) | data formatting | bytes 786432

commit v2 on v1

--- a/solution.py
+++ b/solution.py
@@ -20,6 +20,7 @@
 RIM = 4
 ROWS = NX + 2 * RIM
 NZC, NXC, NYC = NZ // COARSEN, NX // COARSEN, NY // COARSEN
+UNROLL = 8
 F32 = jnp.float32
 NEIGHBOURS = ((1, 0), (-1, 0), (0, 1), (0, -1), (1, 1), (1, -1), (-1, 1), (-1, -1))
 
@@ -98,7 +99,7 @@
                 new.append(jnp.where(window, turned, accs[k]))
             return tuple(new)
 
-        accs = lax.fori_loop(0, 8, step, tuple(jnp.zeros((NX, NY), F32) for _ in range(4)))
+        accs = lax.fori_loop(0, 8, step, tuple(jnp.zeros((NX, NY), F32) for _ in range(4)), unroll=True)
         phase = lax.shift_right_logical(lane24, 2)
 
         def pick(j):
@@ -117,7 +118,7 @@
         extract(i, ref)
     csums = []
     for zc in range(NZC):
-        csums.append(lax.fori_loop(1, COARSEN, lambda i, a, zc=zc: a + C[zc * COARSEN + i, 0:NX], C[zc * COARSEN, 0:NX]))
+        csums.append(functools.reduce(jnp.add, [C[zc * COARSEN + i, 0:NX] for i in range(COARSEN)]))
     CS[...] = tile_of(csums)
 
     pl.semaphore_wait(barrier, len(NEIGHBOURS))
@@ -184,7 +185,7 @@
 
     rsums = []
     for zc in range(NZC):
-        rsums.append(lax.fori_loop(zc * COARSEN, (zc + 1) * COARSEN, setup, jnp.zeros((NX, NY), F32)))
+        rsums.append(lax.fori_loop(zc * COARSEN, (zc + 1) * COARSEN, setup, jnp.zeros((NX, NY), F32), unroll=True))
 
     for copy in strip_copies + cond_copies[:4]:
         copy.wait_recv()
@@ -254,8 +255,8 @@
         U[z] = D[0, z, 0:NX] + c[0:NX] + d[0:NX]
         return carry
 
-    lax.fori_loop(0, NZ, sweep_one, 0)
-    lax.fori_loop(0, NZ, sweep_two, 0)
+    lax.fori_loop(0, NZ, sweep_one, 0, unroll=UNROLL)
+    lax.fori_loop(0, NZ, sweep_two, 0, unroll=UNROLL)
 
     for copy in side_copies + diag_copies:
         copy.wait_recv()
@@ -337,7 +338,7 @@
         o_ref[z] = (V[z, 0:NX] + total) + PR[z // COARSEN]
         return carry
 
-    lax.fori_loop(0, NZ, finish, 0)
+    lax.fori_loop(0, NZ, finish, 0, unroll=UNROLL)
     for copy in near_copies + side_copies + strip_copies + diag_copies + cond_copies + start_copies:
         copy.wait_send()
 

time: 35.7 us -> 29.7 us (0.83)
  Pallas kernels: 33.7 us -> 27.7 us
    pallas_call x1, Pallas kernels: 33.7 us -> 27.7 us  [body(): pl.pallas_call(functools.partial(kernel, sizes), out_shape=jax.ShapeDtype...]
where the time goes in v2:
time: 29.7 us; the launch traced here: 29.5 us
  Pallas kernels  27.7 us (93%)
  local copies, waits for them, and re-layouts  1.77 us (6%)
    pallas_call x1, Pallas kernels, body(): pl.pallas_call(functools.partial(kernel, sizes), out_shape=jax.ShapeDtype...  27.7 us
    unnamed x1, local copies, waits for them, and re-layouts  1.77 us

profile of v2, /device:TPU:1, one launch (start us, length us, event | category | flops | bytes accessed | tf_op | source)
XLA Modules:
  0.0 29.5 jit_solution(15661234477703388251)
XLA Ops:
  0.0 27.7 %shard_map.37 = f32[32,24,128]{2,1,0:T(8,128)} custom-call(f32[32,24,128]{2,1,0:T(8,128)} %v_hbm.1, f32[32,24,128]{2,1,0:T(8,128)} %s_hbm.1, f32[32,24,128]{2,1,0:T(8,128)} %c_hbm.1), custom_call_target="tpu_custom_call" | custom-call | tf_op jit(solution)/shard_map/pallas_call | solution.py:352
  27.7 1.8 %copy.5 = f32[32,24,128]{2,1,0:T(8,128)} copy(f32[32,24,128]{2,1,0:T(8,128)} %shard_map.37) | data formatting | bytes 786432

commit v3 on v2

--- a/solution.py
+++ b/solution.py
@@ -351,7 +351,7 @@
         dma = pltpu.SemaphoreType.DMA
         return pl.pallas_call(
             functools.partial(kernel, sizes),
-            out_shape=jax.ShapeDtypeStruct((NZ, NX, NY), F32),
+            out_shape=pltpu.VMEM((NZ, NX, NY), F32),
             in_specs=[pl.BlockSpec(memory_space=pl.ANY)] * 3,
             out_specs=pl.BlockSpec(memory_space=pltpu.VMEM),
             scratch_shapes=[

time: 29.7 us -> 27.9 us (0.939)
  local copies, waits for them, and re-layouts: 1.77 us -> 0.75 us
  Pallas kernels: 27.7 us -> 27 us
    unnamed x1, local copies, waits for them, and re-layouts: 1.77 us -> 0.75 us
    pallas_call x1, Pallas kernels: 27.7 us -> 27 us  [body(): pl.pallas_call(functools.partial(kernel, sizes), out_shape=pltpu.VMEM((NZ...]
where the time goes in v3:
time: 27.9 us; the launch traced here: 27.7 us
  Pallas kernels  27 us (97%)
  local copies, waits for them, and re-layouts  0.75 us (3%)
    pallas_call x1, Pallas kernels, body(): pl.pallas_call(functools.partial(kernel, sizes), out_shape=pltpu.VMEM((NZ...  27 us
    unnamed x1, local copies, waits for them, and re-layouts  0.75 us

profile of v3, /device:TPU:1, one launch (start us, length us, event | category | flops | bytes accessed | tf_op | source)
XLA Modules:
  0.0 27.7 jit_solution(7752501646140618941)
XLA Ops:
  0.0 27.0 %shard_map.37 = f32[32,24,128]{2,1,0:T(8,128)S(1)} custom-call(f32[32,24,128]{2,1,0:T(8,128)} %v_hbm.1, f32[32,24,128]{2,1,0:T(8,128)} %s_hbm.1, f32[32,24,128]{2,1,0:T(8,128)} %c_hbm.1), custom_call_target="tpu_custom_call" | custom-call | tf_op jit(solution)/shard_map/pallas_call | solution.py:352
  27.0 0.7 %copy.5 = f32[32,24,128]{2,1,0:T(8,128)} copy(f32[32,24,128]{2,1,0:T(8,128)S(1)} %shard_map.37) | data formatting | bytes 786432

commit v4 on v3

--- a/solution.py
+++ b/solution.py
@@ -50,8 +50,8 @@
     return theta, steps
 
 
-def kernel(sizes, v_hbm, s_hbm, c_hbm, o_ref, V, C, S, W, RT, D, U, K, KW, KR, KD, EO, PR, MR, ME, CS, CR, XS, XR,
-           own_sem, fs, fr, ks, kr, cs, cr, xs, xr):
+def kernel(sizes, v_hbm, s_hbm, c_hbm, o_ref, V, C, S, W, RT, D, U, K, KW, KR, KD, EO, MR, ME, CS, CR, XS, XR, TH, TO, PS,
+           own_sem, ts, tr, fs, fr, ks, kr, cs, cr, xs, xr):
     ngx, ngy = sizes
     gx, gy = lax.axis_index("gx"), lax.axis_index("gy")
 
@@ -65,6 +65,12 @@
     for i, (src, dst) in enumerate(((v_hbm, V), (c_hbm, C), (s_hbm, S))):
         loads.append(pltpu.make_async_copy(src, dst.at[:, 0:NX, :], own_sem.at[i]))
         loads[-1].start()
+    edges = []
+    for i, src in enumerate((v_hbm, c_hbm)):
+        edges.append(pltpu.make_async_copy(src.at[:, 0, :], TO.at[0, i], own_sem.at[3 + 2 * i]))
+        edges.append(pltpu.make_async_copy(src.at[:, NX - 1, :], TO.at[1, i], own_sem.at[4 + 2 * i]))
+    for copy in edges:
+        copy.start()
 
     theta, steps = coefficients()
     lane24 = iota((NX, NY), 1)
@@ -86,7 +92,7 @@
     def tile_of(sums):
         out = jnp.zeros((8, NY), F32)
         for zc in range(NZC):
-            out = out + jnp.dot(three_rows(sums[zc]), MR[zc], precision=lax.Precision.HIGHEST, preferred_element_type=F32)
+            out = out + jnp.dot(sums[zc], MR[zc], precision=lax.Precision.HIGHEST, preferred_element_type=F32)
         return out
 
     def extract(f, ref):
@@ -118,8 +124,26 @@
         extract(i, ref)
     csums = []
     for zc in range(NZC):
-        csums.append(functools.reduce(jnp.add, [C[zc * COARSEN + i, 0:NX] for i in range(COARSEN)]))
+        csums.append(three_rows(functools.reduce(jnp.add, [C[zc * COARSEN + i, 0:NX] for i in range(COARSEN)])))
     CS[...] = tile_of(csums)
+
+    row24 = iota((NX, NY), 0)
+    inner = (row24 != NX - 1, row24 != 0, lane24 != NY - 1, lane24 != 0)
+
+    def partial(z, acc):
+        up, dn = (z + 1) & (NZ - 1), (z + NZ - 1) & (NZ - 1)
+        c, v = C[z, 0:NX], V[z, 0:NX]
+        total = (c + C[up, 0:NX]) * (V[up, 0:NX] - v) + (c + C[dn, 0:NX]) * (V[dn, 0:NX] - v)
+        for turn, s, keep in zip((rows, rows, lanes, lanes), (-1, 1, -1, 1), inner):
+            total = total + jnp.where(keep, (c + turn(c, s)) * (turn(v, s) - v), 0.0)
+        return acc + ((S[z, 0:NX] - SHIFT * v) + 0.5 * total)
+
+    for zc in range(NZC):
+        PS[zc] = three_rows(
+            lax.fori_loop(zc * COARSEN, (zc + 1) * COARSEN, partial, jnp.zeros((NX, NY), F32), unroll=True)
+        )
+    for copy in edges:
+        copy.wait()
 
     pl.semaphore_wait(barrier, len(NEIGHBOURS))
 
@@ -132,6 +156,15 @@
 
     low, high = slice(NX, NX + RIM), slice(NX + RIM, ROWS)
     first, last = slice(0, RIM), slice(NX - RIM, NX)
+    thin_copies = []
+    for i, src in enumerate((v_hbm, c_hbm)):
+        thin_copies.append(send(src.at[:, NX - 1, :], TH.at[0, i], ts.at[2 * i], tr.at[2 * i], (1, 0)))
+        thin_copies.append(send(src.at[:, 0, :], TH.at[1, i], ts.at[2 * i + 1], tr.at[2 * i + 1], (-1, 0)))
+    strip_copies = [
+        send(K.at[:, 4, 0:NX], K.at[:, 0, 0:NX], ks.at[2], kr.at[2], (0, 1)),
+        send(K.at[:, 1, 0:NX], K.at[:, 5, 0:NX], ks.at[3], kr.at[3], (0, -1)),
+    ]
+    cond_copies = [send(CS, CR.at[i], cs.at[i], cr.at[i], d) for i, d in enumerate(NEIGHBOURS)]
     diag_copies = [
         send(K.at[:, 4, last], K.at[:, 0, high], ks.at[4], kr.at[4], (1, 1)),
         send(K.at[:, 1, last], K.at[:, 5, high], ks.at[5], kr.at[5], (1, -1)),
@@ -146,19 +179,64 @@
         send(K.at[:, 1:5, last], K.at[:, 1:5, high], ks.at[0], kr.at[0], (1, 0)),
         send(K.at[:, 1:5, first], K.at[:, 1:5, low], ks.at[1], kr.at[1], (-1, 0)),
     ]
-    strip_copies = [
-        send(K.at[:, 4, 0:NX], K.at[:, 0, 0:NX], ks.at[2], kr.at[2], (0, 1)),
-        send(K.at[:, 1, 0:NX], K.at[:, 5, 0:NX], ks.at[3], kr.at[3], (0, -1)),
-    ]
-    cond_copies = [send(CS, CR.at[i], cs.at[i], cr.at[i], d) for i, d in enumerate(NEIGHBOURS)]
-
+
+
+    for copy in thin_copies + strip_copies + cond_copies[:4]:
+        copy.wait_recv()
+    col0 = (lane24 & 3) == 0
+
+    def face(outer, inner, turn_outer, turn_inner):
+        vo, vi, co, ci = K[0, outer, 0:NX], K[0, inner, 0:NX], K[1, outer, 0:NX], K[1, inner, 0:NX]
+        if turn_outer:
+            vo, co = lanes(vo, turn_outer), lanes(co, turn_outer)
+        if turn_inner:
+            vi, ci = lanes(vi, turn_inner), lanes(ci, turn_inner)
+        flux = jnp.where(col0, 0.5 * (co + ci) * (vo - vi), 0.0)
+        for s in (4, 8, 16):
+            flux = flux + lanes(flux, -s)
+        return three_rows(flux) * (1.0 / COARSEN**3)
+
+    def flux_rows(side, row):
+        flux = 0.5 * (TO[side, 1] + TH[side, 1]) * (TH[side, 0] - TO[side, 0])
+        return [
+            jnp.where(row8 == row, jnp.sum(flux[8 * zc : 8 * zc + 8], axis=0, keepdims=True), 0.0) for zc in range(NZC)
+        ]
+
+    below, above = flux_rows(0, 0), flux_rows(1, NXC - 1)
+    rhs = tile_of([PS[zc] + (below[zc] + above[zc]) for zc in range(NZC)])
+    rhs = rhs + jnp.where((lane8 & 31) == 8, lanes(face(0, 1, -3, 0), 8), 0.0)
+    rhs = rhs + jnp.where((lane8 & 31) == 23, lanes(face(5, 4, 0, -3), 23), 0.0)
+
+    spot = lane8 & 31
+
+    def widen(left, centre, right):
+        out = jnp.where((spot >= 8) & (spot < 24), centre, 0.0)
+        if left is not None:
+            out = jnp.where((spot >= 4) & (spot < 8), lanes(left, -16), out)
+            out = jnp.where((spot >= 24) & (spot < 28), lanes(right, 16), out)
+        return out
+
+    def stack(below, centre, above):
+        top = jnp.where(row8 < 3, centre, jnp.where(row8 < 6, rows(above, 3), 0.0))
+        bottom = jnp.where(row8 >= 5, rows(below, 5), 0.0)
+        return jnp.concatenate([top, bottom], axis=0)
+
+    def coarse_weights(c):
+        c = c * (0.5 / COARSEN**2)
+        ws = [c + lanes(c, 32), c + lanes(c, -32), c + rows(c, -1), c + rows(c, 1), c + lanes(c, -1), c + lanes(c, 1)]
+        diag = SHIFT + (((ws[0] + ws[1]) + (ws[2] + ws[3])) + (ws[4] + ws[5]))
+        inv = OMEGA / diag
+        return inv, ws
+
+    own = CS[...]
+    inv, _ = coarse_weights(stack(CR[0], widen(CR[2], own, CR[3]), CR[1]))
+    XS[...] = rhs * inv[0:8]
+    start_copies = [send(XS, XR.at[i], xs.at[i], xr.at[i], d) for i, d in enumerate(NEIGHBOURS)]
 
     for copy in near_copies:
         copy.wait_recv()
-    not_last = lane32 != NY - 1
-    not_first = lane32 != 0
-
-    def setup(z, acc):
+
+    def setup(z, carry):
         up, dn = (z + 1) & (NZ - 1), (z + NZ - 1) & (NZ - 1)
         c, v = C[z], V[z]
         ws = [
@@ -166,8 +244,8 @@
             c + C[dn],
             c + rows(c, -1),
             c + rows(c, 1),
-            jnp.where(not_last, c + lanes(c, -1), 0.0),
-            jnp.where(not_first, c + lanes(c, 1), 0.0),
+            c + lanes(c, -1),
+            c + lanes(c, 1),
         ]
         vs = [V[up], V[dn], rows(v, -1), rows(v, 1), lanes(v, -1), lanes(v, 1)]
         total = ((ws[0] + ws[1]) + (ws[2] + ws[3])) + (ws[4] + ws[5])
@@ -181,56 +259,9 @@
         rt = residual * inv
         RT[z] = rt
         D[0, z] = rt * (1.0 / theta)
-        return acc + residual[0:NX]
-
-    rsums = []
-    for zc in range(NZC):
-        rsums.append(lax.fori_loop(zc * COARSEN, (zc + 1) * COARSEN, setup, jnp.zeros((NX, NY), F32), unroll=True))
-
-    for copy in strip_copies + cond_copies[:4]:
-        copy.wait_recv()
-    col0 = (lane24 & 3) == 0
-
-    def face(outer, inner, turn_outer, turn_inner):
-        vo, vi, co, ci = K[0, outer, 0:NX], K[0, inner, 0:NX], K[1, outer, 0:NX], K[1, inner, 0:NX]
-        if turn_outer:
-            vo, co = lanes(vo, turn_outer), lanes(co, turn_outer)
-        if turn_inner:
-            vi, ci = lanes(vi, turn_inner), lanes(ci, turn_inner)
-        flux = jnp.where(col0, 0.5 * (co + ci) * (vo - vi), 0.0)
-        for s in (4, 8, 16):
-            flux = flux + lanes(flux, -s)
-        return three_rows(flux) * (1.0 / COARSEN**3)
-
-    rhs = tile_of(rsums)
-    rhs = rhs + jnp.where((lane8 & 31) == 8, lanes(face(0, 1, -3, 0), 8), 0.0)
-    rhs = rhs + jnp.where((lane8 & 31) == 23, lanes(face(5, 4, 0, -3), 23), 0.0)
-
-    spot = lane8 & 31
-
-    def widen(left, centre, right):
-        out = jnp.where((spot >= 8) & (spot < 24), centre, 0.0)
-        if left is not None:
-            out = jnp.where((spot >= 4) & (spot < 8), lanes(left, -16), out)
-            out = jnp.where((spot >= 24) & (spot < 28), lanes(right, 16), out)
-        return out
-
-    def stack(below, centre, above):
-        top = jnp.where(row8 < 3, centre, jnp.where(row8 < 6, rows(above, 3), 0.0))
-        bottom = jnp.where(row8 >= 5, rows(below, 5), 0.0)
-        return jnp.concatenate([top, bottom], axis=0)
-
-    def coarse_weights(c):
-        c = c * (0.5 / COARSEN**2)
-        ws = [c + lanes(c, 32), c + lanes(c, -32), c + rows(c, -1), c + rows(c, 1), c + lanes(c, -1), c + lanes(c, 1)]
-        diag = SHIFT + (((ws[0] + ws[1]) + (ws[2] + ws[3])) + (ws[4] + ws[5]))
-        inv = OMEGA / diag
-        return inv, ws
-
-    own = CS[...]
-    inv, _ = coarse_weights(stack(CR[0], widen(CR[2], own, CR[3]), CR[1]))
-    XS[...] = rhs * inv[0:8]
-    start_copies = [send(XS, XR.at[i], xs.at[i], xr.at[i], d) for i, d in enumerate(NEIGHBOURS)]
+        return carry
+
+    lax.fori_loop(0, NZ, setup, 0, unroll=UNROLL)
 
     def image(z, d):
         up, dn = (z + 1) & (NZ - 1), (z + NZ - 1) & (NZ - 1)
@@ -303,7 +334,20 @@
     EO[0] = jnp.where(even, right, left)
     EO[1] = jnp.where(even, left, right)
 
-    for copy in cond_copies[4:] + start_copies:
+    edge = (lane24 < 4) | (lane24 >= NY - 4)
+
+    def finish(z, carry):
+        c, gain = image(z, 2)
+        rt = (RT[z] - c) + gain
+        d = steps[2][0] * c + steps[2][1] * rt
+        total = U[z] + d[0:NX]
+        strip = pltpu.roll(EO[z & 1], (2 * NY - 4 - 4 * z) & (NY - 1), 1)
+        total = jnp.where(edge, strip, total)
+        U[z] = V[z, 0:NX] + total
+        return carry
+
+    lax.fori_loop(0, NZ, finish, 0, unroll=UNROLL)
+    for copy in cond_copies[4:]:
         copy.wait_recv()
 
     def extended(ref, own):
@@ -313,6 +357,8 @@
 
     inv, ws = coarse_weights(extended(CR, own))
     ws = [w * inv for w in ws]
+    for copy in start_copies:
+        copy.wait_recv()
     start = extended(XR, XS[...])
     x = start
     for _ in range(COARSE_SWEEPS - 1):
@@ -323,23 +369,12 @@
     x = x[0:8]
     for zc in range(NZC):
         spread = jnp.dot(x, ME[zc], precision=lax.Precision.HIGHEST, preferred_element_type=F32)
-        for j in range(NXC):
-            PR[zc, 8 * j : 8 * j + 8] = jnp.broadcast_to(spread[j : j + 1], (8, NY))
-
-    edge = (lane24 < 4) | (lane24 >= NY - 4)
-
-    def finish(z, carry):
-        c, gain = image(z, 2)
-        rt = (RT[z] - c) + gain
-        d = steps[2][0] * c + steps[2][1] * rt
-        total = U[z] + d[0:NX]
-        strip = pltpu.roll(EO[z & 1], (2 * NY - 4 - 4 * z) & (NY - 1), 1)
-        total = jnp.where(edge, strip, total)
-        o_ref[z] = (V[z, 0:NX] + total) + PR[z // COARSEN]
-        return carry
-
-    lax.fori_loop(0, NZ, finish, 0, unroll=UNROLL)
-    for copy in near_copies + side_copies + strip_copies + diag_copies + cond_copies + start_copies:
+        wide = [jnp.broadcast_to(spread[j : j + 1], (8, NY)) for j in range(NXC)]
+        for z in range(zc * COARSEN, (zc + 1) * COARSEN):
+            for j in range(NXC):
+                o_ref[z, 8 * j : 8 * j + 8] = U[z, 8 * j : 8 * j + 8] + wide[j]
+
+    for copy in thin_copies + near_copies + side_copies + strip_copies + diag_copies + cond_copies + start_copies:
         copy.wait_send()
 
 
@@ -367,14 +402,18 @@
                 pltpu.VMEM((6, ROWS, NY), F32),
                 pltpu.VMEM((4, 6, ROWS, NY), F32),
                 pltpu.VMEM((2, NX, NY), F32),
-                pltpu.VMEM((NZC, NX, NY), F32),
                 pltpu.VMEM((NZC, NY, NY), F32),
                 pltpu.VMEM((NZC, NY, NY), F32),
                 pltpu.VMEM((8, NY), F32),
                 pltpu.VMEM((8, 8, NY), F32),
                 pltpu.VMEM((8, NY), F32),
                 pltpu.VMEM((8, 8, NY), F32),
-                dma((3,)),
+                pltpu.VMEM((2, 2, NZ, NY), F32),
+                pltpu.VMEM((2, 2, NZ, NY), F32),
+                pltpu.VMEM((NZC, 8, NY), F32),
+                dma((7,)),
+                dma((4,)),
+                dma((4,)),
                 dma((6,)),
                 dma((6,)),
                 dma((8,)),

time: 27.9 us -> 26.4 us (0.946)
  Pallas kernels: 27 us -> 25.5 us
    pallas_call x1, Pallas kernels: 27 us -> 25.5 us  [body(): pl.pallas_call(functools.partial(kernel, sizes), out_shape=pltpu.VMEM((NZ...]
where the time goes in v4:
time: 26.4 us; the launch traced here: 26.3 us
  Pallas kernels  25.5 us (97%)
  local copies, waits for them, and re-layouts  0.75 us (3%)
    pallas_call x1, Pallas kernels, body(): pl.pallas_call(functools.partial(kernel, sizes), out_shape=pltpu.VMEM((NZ...  25.5 us
    unnamed x1, local copies, waits for them, and re-layouts  0.75 us

profile of v4, /device:TPU:1, one launch (start us, length us, event | category | flops | bytes accessed | tf_op | source)
XLA Modules:
  0.0 26.3 jit_solution(13496444883368625009)
XLA Ops:
  0.0 25.5 %shard_map.37 = f32[32,24,128]{2,1,0:T(8,128)S(1)} custom-call(f32[32,24,128]{2,1,0:T(8,128)} %v_hbm.1, f32[32,24,128]{2,1,0:T(8,128)} %s_hbm.1, f32[32,24,128]{2,1,0:T(8,128)} %c_hbm.1), custom_call_target="tpu_custom_call" | custom-call | tf_op jit(solution)/shard_map/pallas_call | solution.py:387
  25.5 0.7 %copy.5 = f32[32,24,128]{2,1,0:T(8,128)} copy(f32[32,24,128]{2,1,0:T(8,128)S(1)} %shard_map.37) | data formatting | bytes 786432

commit v5 on v4

--- a/solution.py
+++ b/solution.py
@@ -50,8 +50,8 @@
     return theta, steps
 
 
-def kernel(sizes, v_hbm, s_hbm, c_hbm, o_ref, V, C, S, W, RT, D, U, K, KW, KR, KD, EO, MR, ME, CS, CR, XS, XR, TH, TO, PS,
-           own_sem, ts, tr, fs, fr, ks, kr, cs, cr, xs, xr):
+def kernel(sizes, v_hbm, s_hbm, c_hbm, o_ref, V, C, S, W, RT, D, U, K, KW, KR, KD, EO, MR, ME, CS, CR, XS, XR, TH, TO, PT, KX, PX, AC, AX, FB, FX, XB,
+           own_sem, go, ls, lr, ts, tr, fs, fr, ks, kr, cs, cr, xs, xr):
     ngx, ngy = sizes
     gx, gy = lax.axis_index("gx"), lax.axis_index("gy")
 
@@ -59,8 +59,18 @@
         return (lax.rem(gx + d[0] + ngx, ngx), lax.rem(gy + d[1] + ngy, ngy))
 
     barrier = pltpu.get_barrier_semaphore()
+    is_last, is_first = gx == ngx - 1, gx == 0
     for d in NEIGHBOURS:
-        pl.semaphore_signal(barrier, inc=1, device_id=at(d), device_id_type=MESH)
+
+        def greet(d=d):
+            pl.semaphore_signal(barrier, inc=1, device_id=at(d), device_id_type=MESH)
+
+        if d[0] == 1:
+            pl.when(gx < ngx - 2)(greet)
+        elif d[0] == 0:
+            pl.when(gx != ngx - 1)(greet)
+        else:
+            greet()
     loads = []
     for i, (src, dst) in enumerate(((v_hbm, V), (c_hbm, C), (s_hbm, S))):
         loads.append(pltpu.make_async_copy(src, dst.at[:, 0:NX, :], own_sem.at[i]))
@@ -72,6 +82,51 @@
     for copy in edges:
         copy.start()
 
+    def remote(src, dst, send_sem, recv_sem, d):
+        return pltpu.make_async_remote_copy(
+            src_ref=src, dst_ref=dst, send_sem=send_sem, recv_sem=recv_sem, device_id=at(d), device_id_type=MESH
+        )
+
+    low, high = slice(NX, NX + RIM), slice(NX + RIM, ROWS)
+    first, last = slice(0, RIM), slice(NX - RIM, NX)
+    thin_copies = []
+    for i, src in enumerate((v_hbm, c_hbm)):
+        thin_copies.append(remote(src.at[:, NX - 1, :], TH.at[0, i], ts.at[2 * i], tr.at[2 * i], (1, 0)))
+        thin_copies.append(remote(src.at[:, 0, :], TH.at[1, i], ts.at[2 * i + 1], tr.at[2 * i + 1], (-1, 0)))
+    strip_copies = [
+        remote(K.at[:, 4, 0:NX], K.at[:, 0, 0:NX], ks.at[2], kr.at[2], (0, 1)),
+        remote(K.at[:, 1, 0:NX], K.at[:, 5, 0:NX], ks.at[3], kr.at[3], (0, -1)),
+    ]
+    cond_copies = [remote(CS, CR.at[i], cs.at[i], cr.at[i], d) for i, d in enumerate(NEIGHBOURS)]
+    diag_copies = [
+        remote(K.at[:, 4, last], K.at[:, 0, high], ks.at[4], kr.at[4], (1, 1)),
+        remote(K.at[:, 1, last], K.at[:, 5, high], ks.at[5], kr.at[5], (1, -1)),
+        remote(K.at[:, 4, first], K.at[:, 0, low], ks.at[6], kr.at[6], (-1, 1)),
+        remote(K.at[:, 1, first], K.at[:, 5, low], ks.at[7], kr.at[7], (-1, -1)),
+    ]
+    near_copies = []
+    for i, (src, dst) in enumerate(((v_hbm, V), (c_hbm, C), (s_hbm, S))):
+        near_copies.append(remote(src.at[:, last, :], dst.at[:, high, :], fs.at[2 * i], fr.at[2 * i], (1, 0)))
+        near_copies.append(remote(src.at[:, first, :], dst.at[:, low, :], fs.at[2 * i + 1], fr.at[2 * i + 1], (-1, 0)))
+    side_copies = [
+        remote(K.at[:, 1:5, last], K.at[:, 1:5, high], ks.at[0], kr.at[0], (1, 0)),
+        remote(K.at[:, 1:5, first], K.at[:, 1:5, low], ks.at[1], kr.at[1], (-1, 0)),
+    ]
+
+    def start(copies):
+        for copy in copies:
+            copy.start()
+
+    up_rows = thin_copies[0::2] + near_copies[0::2]
+    up_local = diag_copies[0:2] + [cond_copies[0], cond_copies[4], cond_copies[5], side_copies[0]]
+
+    @pl.when(is_last)
+    def _():
+        pl.semaphore_wait(barrier, 3)
+        for d in ((1, 0), (1, 1), (1, -1)):
+            pl.semaphore_signal(go, inc=1, device_id=at(d), device_id_type=MESH)
+        start(up_rows)
+
     theta, steps = coefficients()
     lane24 = iota((NX, NY), 1)
     lane32 = iota((ROWS, NY), 1)
@@ -127,6 +182,10 @@
         csums.append(three_rows(functools.reduce(jnp.add, [C[zc * COARSEN + i, 0:NX] for i in range(COARSEN)])))
     CS[...] = tile_of(csums)
 
+    @pl.when(is_last)
+    def _():
+        start(up_local)
+
     row24 = iota((NX, NY), 0)
     inner = (row24 != NX - 1, row24 != 0, lane24 != NY - 1, lane24 != 0)
 
@@ -138,55 +197,79 @@
             total = total + jnp.where(keep, (c + turn(c, s)) * (turn(v, s) - v), 0.0)
         return acc + ((S[z, 0:NX] - SHIFT * v) + 0.5 * total)
 
-    for zc in range(NZC):
-        PS[zc] = three_rows(
-            lax.fori_loop(zc * COARSEN, (zc + 1) * COARSEN, partial, jnp.zeros((NX, NY), F32), unroll=True)
-        )
+    PT[...] = tile_of(
+        [
+            three_rows(
+                lax.fori_loop(zc * COARSEN, (zc + 1) * COARSEN, partial, jnp.zeros((NX, NY), F32), unroll=True)
+            )
+            for zc in range(NZC)
+        ]
+    )
+    strips_up = [
+        remote(K.at[0:2, 1, 0:NX], KX.at[0], ls.at[0], lr.at[0], (1, 0)),
+        remote(K.at[0:2, 4, 0:NX], KX.at[1], ls.at[1], lr.at[1], (1, 0)),
+        remote(K.at[0:2, 4, 0:NX], KX.at[2], ls.at[2], lr.at[2], (1, 1)),
+        remote(K.at[0:2, 1, 0:NX], KX.at[3], ls.at[3], lr.at[3], (1, -1)),
+        remote(PT, PX.at[0], ls.at[4], lr.at[4], (1, 1)),
+        remote(PT, PX.at[1], ls.at[5], lr.at[5], (1, -1)),
+    ]
+    tile_up = remote(AC, AX, ls.at[6], lr.at[6], (1, 0))
+    face_sides = [remote(FB, FX.at[0], ls.at[7], lr.at[7], (0, 1)), remote(FB, FX.at[1], ls.at[8], lr.at[8], (0, -1))]
+
+    @pl.when(is_last)
+    def _():
+        start(strips_up)
+
     for copy in edges:
         copy.wait()
 
-    pl.semaphore_wait(barrier, len(NEIGHBOURS))
-
-    def send(src, dst, send_sem, recv_sem, d):
-        copy = pltpu.make_async_remote_copy(
-            src_ref=src, dst_ref=dst, send_sem=send_sem, recv_sem=recv_sem, device_id=at(d), device_id_type=MESH
+    down = thin_copies[1::2] + [cond_copies[i] for i in (1, 6, 7)] + diag_copies[2:] + near_copies[1::2] + side_copies[1:]
+    side = strip_copies + cond_copies[2:4]
+
+    @pl.when(is_last)
+    def _():
+        pl.semaphore_wait(go, 1)
+        start(side + down)
+
+    @pl.when(is_first)
+    def _():
+        pl.semaphore_wait(barrier, 5)
+        start(side + up_rows + up_local)
+
+    @pl.when(jnp.logical_not(is_last | is_first))
+    def _():
+        pl.semaphore_wait(barrier, len(NEIGHBOURS))
+
+        @pl.when(gx == ngx - 2)
+        def _():
+            pl.semaphore_signal(go, inc=1, device_id=at((1, 0)), device_id_type=MESH)
+
+        start(thin_copies + strip_copies + cond_copies + diag_copies + near_copies + side_copies)
+
+
+    def flux_tile(side, row):
+        flux = 0.5 * (TO[side, 1] + TH[side, 1]) * (TH[side, 0] - TO[side, 0])
+        return tile_of(
+            [jnp.where(row8 == row, jnp.sum(flux[8 * zc : 8 * zc + 8], axis=0, keepdims=True), 0.0) for zc in range(NZC)]
         )
-        copy.start()
-        return copy
-
-    low, high = slice(NX, NX + RIM), slice(NX + RIM, ROWS)
-    first, last = slice(0, RIM), slice(NX - RIM, NX)
-    thin_copies = []
-    for i, src in enumerate((v_hbm, c_hbm)):
-        thin_copies.append(send(src.at[:, NX - 1, :], TH.at[0, i], ts.at[2 * i], tr.at[2 * i], (1, 0)))
-        thin_copies.append(send(src.at[:, 0, :], TH.at[1, i], ts.at[2 * i + 1], tr.at[2 * i + 1], (-1, 0)))
-    strip_copies = [
-        send(K.at[:, 4, 0:NX], K.at[:, 0, 0:NX], ks.at[2], kr.at[2], (0, 1)),
-        send(K.at[:, 1, 0:NX], K.at[:, 5, 0:NX], ks.at[3], kr.at[3], (0, -1)),
-    ]
-    cond_copies = [send(CS, CR.at[i], cs.at[i], cr.at[i], d) for i, d in enumerate(NEIGHBOURS)]
-    diag_copies = [
-        send(K.at[:, 4, last], K.at[:, 0, high], ks.at[4], kr.at[4], (1, 1)),
-        send(K.at[:, 1, last], K.at[:, 5, high], ks.at[5], kr.at[5], (1, -1)),
-        send(K.at[:, 4, first], K.at[:, 0, low], ks.at[6], kr.at[6], (-1, 1)),
-        send(K.at[:, 1, first], K.at[:, 5, low], ks.at[7], kr.at[7], (-1, -1)),
-    ]
-    near_copies = []
-    for i, (src, dst) in enumerate(((v_hbm, V), (c_hbm, C), (s_hbm, S))):
-        near_copies.append(send(src.at[:, last, :], dst.at[:, high, :], fs.at[2 * i], fr.at[2 * i], (1, 0)))
-        near_copies.append(send(src.at[:, first, :], dst.at[:, low, :], fs.at[2 * i + 1], fr.at[2 * i + 1], (-1, 0)))
-    side_copies = [
-        send(K.at[:, 1:5, last], K.at[:, 1:5, high], ks.at[0], kr.at[0], (1, 0)),
-        send(K.at[:, 1:5, first], K.at[:, 1:5, low], ks.at[1], kr.at[1], (-1, 0)),
-    ]
-
-
-    for copy in thin_copies + strip_copies + cond_copies[:4]:
+
+    def take_below():
+        for copy in thin_copies[0::2] + cond_copies[:1]:
+            copy.wait_recv()
+        FB[...] = flux_tile(0, 0)
+
+    @pl.when(is_last)
+    def _():
+        take_below()
+        AC[0] = PT[...] + FB[...]
+        AC[1] = CR[0]
+        tile_up.start()
+
+    for copy in thin_copies[1::2] + strip_copies + cond_copies[1:4]:
         copy.wait_recv()
     col0 = (lane24 & 3) == 0
 
-    def face(outer, inner, turn_outer, turn_inner):
-        vo, vi, co, ci = K[0, outer, 0:NX], K[0, inner, 0:NX], K[1, outer, 0:NX], K[1, inner, 0:NX]
+    def face(vo, co, vi, ci, turn_outer, turn_inner):
         if turn_outer:
             vo, co = lanes(vo, turn_outer), lanes(co, turn_outer)
         if turn_inner:
@@ -196,16 +279,13 @@
             flux = flux + lanes(flux, -s)
         return three_rows(flux) * (1.0 / COARSEN**3)
 
-    def flux_rows(side, row):
-        flux = 0.5 * (TO[side, 1] + TH[side, 1]) * (TH[side, 0] - TO[side, 0])
-        return [
-            jnp.where(row8 == row, jnp.sum(flux[8 * zc : 8 * zc + 8], axis=0, keepdims=True), 0.0) for zc in range(NZC)
-        ]
-
-    below, above = flux_rows(0, 0), flux_rows(1, NXC - 1)
-    rhs = tile_of([PS[zc] + (below[zc] + above[zc]) for zc in range(NZC)])
-    rhs = rhs + jnp.where((lane8 & 31) == 8, lanes(face(0, 1, -3, 0), 8), 0.0)
-    rhs = rhs + jnp.where((lane8 & 31) == 23, lanes(face(5, 4, 0, -3), 23), 0.0)
+    own_strip = lambda g: (K[0, g, 0:NX], K[1, g, 0:NX])
+    far_strip = lambda g: (KX[g, 0], KX[g, 1])
+    at_left = lambda x: jnp.where((lane8 & 31) == 8, lanes(x, 8), 0.0)
+    at_right = lambda x: jnp.where((lane8 & 31) == 23, lanes(x, 23), 0.0)
+    rhs = PT[...] + flux_tile(1, NXC - 1)
+    rhs = rhs + at_left(face(*own_strip(0), *own_strip(1), -3, 0))
+    rhs = rhs + at_right(face(*own_strip(5), *own_strip(4), 0, -3))
 
     spot = lane8 & 31
 
@@ -228,10 +308,31 @@
         inv = OMEGA / diag
         return inv, ws
 
+    @pl.when(jnp.logical_not(is_last))
+    def _():
+        take_below()
+
     own = CS[...]
     inv, _ = coarse_weights(stack(CR[0], widen(CR[2], own, CR[3]), CR[1]))
-    XS[...] = rhs * inv[0:8]
-    start_copies = [send(XS, XR.at[i], xs.at[i], xr.at[i], d) for i, d in enumerate(NEIGHBOURS)]
+    XS[...] = (rhs + FB[...]) * inv[0:8]
+    start_copies = [remote(XS, XR.at[i], xs.at[i], xr.at[i], d) for i, d in enumerate(NEIGHBOURS)]
+    start_up = [start_copies[i] for i in (0, 4, 5)]
+    start_rest = [start_copies[i] for i in (1, 2, 3, 6, 7)]
+
+    @pl.when(jnp.logical_not(is_last))
+    def _():
+        start(start_up)
+
+    start(start_rest[1:3])
+
+    @pl.when(is_first)
+    def _():
+        start(face_sides)
+        pl.semaphore_wait(go, 3)
+        start(down)
+
+    start(start_rest[:1] + start_rest[3:])
+
 
     for copy in near_copies:
         copy.wait_recv()
@@ -350,22 +451,45 @@
     for copy in cond_copies[4:]:
         copy.wait_recv()
 
-    def extended(ref, own):
-        return stack(
-            widen(ref[4], ref[0], ref[5]), widen(ref[2], own, ref[3]), widen(ref[6], ref[1], ref[7])
-        )
-
-    inv, ws = coarse_weights(extended(CR, own))
+    def bottom_of(x):
+        return jnp.where(row8 >= 5, rows(x, 5), 0.0)
+
+    def top_of(ref, own):
+        above = widen(ref[6], ref[1], ref[7])
+        return jnp.where(row8 < 3, widen(ref[2], own, ref[3]), jnp.where(row8 < 6, rows(above, 3), 0.0))
+
+    cond_top, cond_bottom = top_of(CR, own), bottom_of(widen(CR[4], CR[0], CR[5]))
+    inv, ws = coarse_weights(jnp.concatenate([cond_top, cond_bottom], axis=0))
     ws = [w * inv for w in ws]
-    for copy in start_copies:
+
+    @pl.when(is_first)
+    def _():
+        for copy in strips_up + [tile_up] + face_sides:
+            copy.wait_recv()
+        further = jnp.where(row8 == 4, rows(widen(None, AX[1], None), 2), cond_bottom)
+        inv, _ = coarse_weights(jnp.concatenate([cond_top, further], axis=0))
+        left = face(*far_strip(2), *far_strip(0), -3, 0)
+        right = face(*far_strip(3), *far_strip(1), 0, -3)
+        centre = ((AX[0] + at_left(left)) + at_right(right)) - rows(FB[...], 2)
+        before = (PX[0] - at_right(left)) - rows(FX[0], 2)
+        after = (PX[1] - at_left(right)) - rows(FX[1], 2)
+        XB[...] = bottom_of(widen(before, centre, after)) * inv[8:16]
+
+    @pl.when(jnp.logical_not(is_first))
+    def _():
+        for copy in start_up:
+            copy.wait_recv()
+        XB[...] = bottom_of(widen(XR[4], XR[0], XR[5]))
+
+    for copy in start_rest:
         copy.wait_recv()
-    start = extended(XR, XS[...])
-    x = start
+    first_x = jnp.concatenate([top_of(XR, XS[...]), XB[...]], axis=0)
+    x = first_x
     for _ in range(COARSE_SWEEPS - 1):
         near = [lanes(x, 32), lanes(x, -32), rows(x, -1), rows(x, 1), lanes(x, -1), lanes(x, 1)]
         terms = [ws[i] * near[i] for i in range(6)]
         gain = ((terms[0] + terms[1]) + (terms[2] + terms[3])) + (terms[4] + terms[5])
-        x = (start + (1.0 - OMEGA) * x) + gain
+        x = (first_x + (1.0 - OMEGA) * x) + gain
     x = x[0:8]
     for zc in range(NZC):
         spread = jnp.dot(x, ME[zc], precision=lax.Precision.HIGHEST, preferred_element_type=F32)
@@ -374,8 +498,23 @@
             for j in range(NXC):
                 o_ref[z, 8 * j : 8 * j + 8] = U[z, 8 * j : 8 * j + 8] + wide[j]
 
-    for copy in thin_copies + near_copies + side_copies + strip_copies + diag_copies + cond_copies + start_copies:
+    for copy in thin_copies + near_copies + side_copies + strip_copies + diag_copies + cond_copies + start_rest:
         copy.wait_send()
+
+    @pl.when(is_first)
+    def _():
+        for copy in face_sides:
+            copy.wait_send()
+
+    @pl.when(is_last)
+    def _():
+        for copy in strips_up + [tile_up]:
+            copy.wait_send()
+
+    @pl.when(jnp.logical_not(is_last))
+    def _():
+        for copy in start_up:
+            copy.wait_send()
 
 
 def solution(mesh):
@@ -410,8 +549,18 @@
                 pltpu.VMEM((8, 8, NY), F32),
                 pltpu.VMEM((2, 2, NZ, NY), F32),
                 pltpu.VMEM((2, 2, NZ, NY), F32),
-                pltpu.VMEM((NZC, 8, NY), F32),
+                pltpu.VMEM((8, NY), F32),
+                pltpu.VMEM((4, 2, NX, NY), F32),
+                pltpu.VMEM((2, 8, NY), F32),
+                pltpu.VMEM((2, 8, NY), F32),
+                pltpu.VMEM((2, 8, NY), F32),
+                pltpu.VMEM((8, NY), F32),
+                pltpu.VMEM((2, 8, NY), F32),
+                pltpu.VMEM((8, NY), F32),
                 dma((7,)),
+                pltpu.SemaphoreType.REGULAR,
+                dma((9,)),
+                dma((9,)),
                 dma((4,)),
                 dma((4,)),
                 dma((6,)),

time: 26.4 us -> 24.9 us (0.943)
  Pallas kernels: 25.5 us -> 24 us
    pallas_call x1, Pallas kernels: 25.5 us -> 24 us  [body(): pl.pallas_call(functools.partial(kernel, sizes), out_shape=pltpu.VMEM((NZ...]
where the time goes in v5:
time: 24.9 us; the launch traced here: 24.8 us
  Pallas kernels  24 us (96%)
  local copies, waits for them, and re-layouts  0.75 us (3%)
    pallas_call x1, Pallas kernels, body(): pl.pallas_call(functools.partial(kernel, sizes), out_shape=pltpu.VMEM((NZ...  24 us
    unnamed x1, local copies, waits for them, and re-layouts  0.75 us

profile of v5, /device:TPU:1, one launch (start us, length us, event | category | flops | bytes accessed | tf_op | source)
XLA Modules:
  0.0 24.8 jit_solution(2014602497426360199)
XLA Ops:
  0.0 24.0 %shard_map.37 = f32[32,24,128]{2,1,0:T(8,128)S(1)} custom-call(f32[32,24,128]{2,1,0:T(8,128)} %v_hbm.1, f32[32,24,128]{2,1,0:T(8,128)} %s_hbm.1, f32[32,24,128]{2,1,0:T(8,128)} %c_hbm.1), custom_call_target="tpu_custom_call" | custom-call | tf_op jit(solution)/shard_map/pallas_call | solution.py:526
  24.0 0.7 %copy.5 = f32[32,24,128]{2,1,0:T(8,128)} copy(f32[32,24,128]{2,1,0:T(8,128)S(1)} %shard_map.37) | data formatting | bytes 786432

commit v6 on v5

--- a/solution.py
+++ b/solution.py
@@ -50,7 +50,7 @@
     return theta, steps
 
 
-def kernel(sizes, v_hbm, s_hbm, c_hbm, o_ref, V, C, S, W, RT, D, U, K, KW, KR, KD, EO, MR, ME, CS, CR, XS, XR, TH, TO, PT, KX, PX, AC, AX, FB, FX, XB,
+def kernel(sizes, v_hbm, s_hbm, c_hbm, U, PR, V, C, S, W, RT, D, K, KW, KR, KD, EO, MR, ME, CS, CR, XS, XR, TH, TO, PT, KX, PX, AC, AX, FB, FX, XB,
            own_sem, go, ls, lr, ts, tr, fs, fr, ks, kr, cs, cr, xs, xr):
     ngx, ngy = sizes
     gx, gy = lax.axis_index("gx"), lax.axis_index("gy")
@@ -72,7 +72,7 @@
         else:
             greet()
     loads = []
-    for i, (src, dst) in enumerate(((v_hbm, V), (c_hbm, C), (s_hbm, S))):
+    for i, (src, dst) in enumerate(((c_hbm, C), (v_hbm, V), (s_hbm, S))):
         loads.append(pltpu.make_async_copy(src, dst.at[:, 0:NX, :], own_sem.at[i]))
         loads[-1].start()
     edges = []
@@ -105,9 +105,10 @@
         remote(K.at[:, 1, first], K.at[:, 5, low], ks.at[7], kr.at[7], (-1, -1)),
     ]
     near_copies = []
-    for i, (src, dst) in enumerate(((v_hbm, V), (c_hbm, C), (s_hbm, S))):
-        near_copies.append(remote(src.at[:, last, :], dst.at[:, high, :], fs.at[2 * i], fr.at[2 * i], (1, 0)))
-        near_copies.append(remote(src.at[:, first, :], dst.at[:, low, :], fs.at[2 * i + 1], fr.at[2 * i + 1], (-1, 0)))
+    for i, (src, dst, n) in enumerate(((v_hbm, V, RIM), (c_hbm, C, RIM), (s_hbm, S, RIM - 1))):
+        upper, lower = (src.at[:, NX - n : NX, :], dst.at[:, ROWS - n : ROWS, :]), (src.at[:, 0:n, :], dst.at[:, NX : NX + n, :])
+        near_copies.append(remote(*upper, fs.at[2 * i], fr.at[2 * i], (1, 0)))
+        near_copies.append(remote(*lower, fs.at[2 * i + 1], fr.at[2 * i + 1], (-1, 0)))
     side_copies = [
         remote(K.at[:, 1:5, last], K.at[:, 1:5, high], ks.at[0], kr.at[0], (1, 0)),
         remote(K.at[:, 1:5, first], K.at[:, 1:5, low], ks.at[1], kr.at[1], (-1, 0)),
@@ -117,15 +118,15 @@
         for copy in copies:
             copy.start()
 
-    up_rows = thin_copies[0::2] + near_copies[0::2]
-    up_local = diag_copies[0:2] + [cond_copies[0], cond_copies[4], cond_copies[5], side_copies[0]]
+    up_thin, up_rows = thin_copies[0::2], near_copies[0::2]
+    up_local = diag_copies[0:2] + side_copies[:1]
 
     @pl.when(is_last)
     def _():
         pl.semaphore_wait(barrier, 3)
         for d in ((1, 0), (1, 1), (1, -1)):
             pl.semaphore_signal(go, inc=1, device_id=at(d), device_id_type=MESH)
-        start(up_rows)
+        start(up_thin)
 
     theta, steps = coefficients()
     lane24 = iota((NX, NY), 1)
@@ -174,13 +175,20 @@
         K[f, 4, 0:NX] = lanes(pick(1), 4)
         K[f, 3, 0:NX] = lanes(pick(2), 8)
 
-    for i, ref in enumerate((V, C, S)):
-        loads[i].wait()
-        extract(i, ref)
+    loads[0].wait()
     csums = []
     for zc in range(NZC):
         csums.append(three_rows(functools.reduce(jnp.add, [C[zc * COARSEN + i, 0:NX] for i in range(COARSEN)])))
     CS[...] = tile_of(csums)
+
+    @pl.when(is_last)
+    def _():
+        start([cond_copies[i] for i in (0, 4, 5)] + up_rows)
+
+    for i, (f, ref) in enumerate(((1, C), (0, V), (2, S))):
+        if i:
+            loads[i].wait()
+        extract(f, ref)
 
     @pl.when(is_last)
     def _():
@@ -234,7 +242,7 @@
     @pl.when(is_first)
     def _():
         pl.semaphore_wait(barrier, 5)
-        start(side + up_rows + up_local)
+        start(side + [cond_copies[i] for i in (0, 4, 5)] + up_thin + up_rows + up_local)
 
     @pl.when(jnp.logical_not(is_last | is_first))
     def _():
@@ -493,10 +501,8 @@
     x = x[0:8]
     for zc in range(NZC):
         spread = jnp.dot(x, ME[zc], precision=lax.Precision.HIGHEST, preferred_element_type=F32)
-        wide = [jnp.broadcast_to(spread[j : j + 1], (8, NY)) for j in range(NXC)]
-        for z in range(zc * COARSEN, (zc + 1) * COARSEN):
-            for j in range(NXC):
-                o_ref[z, 8 * j : 8 * j + 8] = U[z, 8 * j : 8 * j + 8] + wide[j]
+        for j in range(NXC):
+            PR[zc, 8 * j : 8 * j + 8] = jnp.broadcast_to(spread[j : j + 1], (8, NY))
 
     for copy in thin_copies + near_copies + side_copies + strip_copies + diag_copies + cond_copies + start_rest:
         copy.wait_send()
@@ -523,11 +529,11 @@
     def body(iterate, source, conduct):
         plane = (NZ, ROWS, NY)
         dma = pltpu.SemaphoreType.DMA
-        return pl.pallas_call(
+        fine, coarse = pl.pallas_call(
             functools.partial(kernel, sizes),
-            out_shape=pltpu.VMEM((NZ, NX, NY), F32),
+            out_shape=(pltpu.VMEM((NZ, NX, NY), F32), pltpu.VMEM((NZC, NX, NY), F32)),
             in_specs=[pl.BlockSpec(memory_space=pl.ANY)] * 3,
-            out_specs=pl.BlockSpec(memory_space=pltpu.VMEM),
+            out_specs=(pl.BlockSpec(memory_space=pltpu.VMEM),) * 2,
             scratch_shapes=[
                 pltpu.VMEM(plane, F32),
                 pltpu.VMEM(plane, F32),
@@ -535,7 +541,6 @@
                 pltpu.VMEM((6,) + plane, F32),
                 pltpu.VMEM(plane, F32),
                 pltpu.VMEM((3,) + plane, F32),
-                pltpu.VMEM((NZ, NX, NY), F32),
                 pltpu.VMEM((3, 6, ROWS, NY), F32),
                 pltpu.VMEM((6, 6, ROWS, NY), F32),
                 pltpu.VMEM((6, ROWS, NY), F32),
@@ -574,6 +579,8 @@
             ],
             compiler_params=pltpu.CompilerParams(collective_id=0, has_side_effects=True),
         )(iterate, source, conduct)
+        fine = fine.reshape(NZC, COARSEN, NX, NY)
+        return (fine + coarse[:, None]).reshape(NZ, NX, NY)
 
     return jax.shard_map(
         body,

time: 24.9 us -> 24.2 us (0.972)
  other arithmetic: 0 us -> 0.78 us
  local copies, waits for them, and re-layouts: 0.75 us -> 0 us
  Pallas kernels: 24 us -> 23.3 us
    add x0 -> x1, other arithmetic: none -> 0.78 us  [body(): return (fine + coarse[:, None]).reshape(NZ, NX, NY)]
    unnamed x1 -> x0, local copies, waits for them, and re-layouts: 0.75 us -> none
    pallas_call x1, Pallas kernels: 24 us -> 23.3 us  [body(): pl.pallas_call(functools.partial(kernel, sizes), out_shape=(pltpu.VMEM((N...]
where the time goes in v6:
time: 24.2 us; the launch traced here: 24.1 us
  Pallas kernels  23.3 us (96%)
  other arithmetic  0.78 us (3%)
    pallas_call x1, Pallas kernels, body(): pl.pallas_call(functools.partial(kernel, sizes), out_shape=(pltpu.VMEM((N...  23.3 us
    add x1, other arithmetic, body(): return (fine + coarse[:, None]).reshape(NZ, NX, NY)  0.78 us

profile of v6, /device:TPU:1, one launch (start us, length us, event | category | flops | bytes accessed | tf_op | source)
XLA Modules:
  0.0 24.1 jit_solution(10630530684677596107)
XLA Ops:
  0.0 23.3 %shard_map.37 = (f32[32,24,128]{2,1,0:T(8,128)S(1)}, f32[4,24,128]{2,1,0:T(8,128)S(1)}) custom-call(f32[32,24,128]{2,1,0:T(8,128)} %v_hbm.1, f32[32,24,128]{2,1,0:T(8,128)} %s_hbm.1, f32[32,24,128]{2,1,0:T(8,128)} %c_hbm.1), custom_call_target="tpu_custom_call" | custom-call | tf_op jit(solution)/shard_map/pallas_call | solution.py:532
  23.3 0.8 %bitcast_add_fusion = f32[32,24,128]{2,1,0:T(8,128)} fusion(f32[32,24,128]{2,1,0:T(8,128)S(1)} %get-tuple-element.7, f32[4,24,128]{2,1,0:T(8,128)S(1)} %get-tuple-element.8), kind=kLoop, calls=%fused_computation | loop fusion | flops 98304 | bytes 835584 | tf_op jit(solution)/shard_map/add | solution.py:583
